TPU v7x, 512 devices: a whole 4x4x16 slice. The times are simulated.
512 devices in a mesh: ctx: 64 (over z, y_lo, core), head: 4 (over x), dp: 2 (over y_hi).
Axes of the slice: x: 4, y: 4 (y_hi: 2, y_lo: 2; y = y_hi * 2 + y_lo), z: 16, core: 2. Of those that a mesh axis runs over, the one named last changes fastest.
Arguments:
- values: bfloat16 [2, 8192, 4096], P('dp', 'ctx', 'head'), may hold values from -6 to 6
- dt_raw: float32 [2, 8192, 64], P('dp', 'ctx', 'head'), may hold values from -4 to 4
- dt_bias: float32 [64], P('head'), may hold values from -8 to -2
- decay_rate: float32 [64], P('head'), may hold values from 0 to 50, as said below
- features: bfloat16 [2, 8192, 8192], P('dp', 'ctx', 'head'), may hold values from -6 to 6
- bc_weight: bfloat16 [8192, 256], P('head'), may hold values from -0.0625 to 0.0625
- out_grad: bfloat16 [2, 8192, 4096], P('dp', 'ctx', 'head'), may hold values from -6 to 6
Outputs:
- grad_values: bfloat16 [2, 8192, 4096], P('dp', 'ctx', 'head')
- grad_dt: float32 [2, 8192, 64], P('dp', 'ctx', 'head')
- grad_features: bfloat16 [2, 8192, 8192], P('dp', 'ctx', 'head')
- grad_weight: float32 [256, 8192], P(('ctx', 'dp'), 'head')
Inputs may be any that keep to these rules, and one draw needn't show every extreme that they name: `decay_rate`: positive.
All inputs are finite; a program needn't handle non-finite values.
Results may differ from a plain program's by a relative error of at most 0.014.
Values may be sent and summed in bfloat16 or wider, within the bound.
A program may use at most 192 MiB of HBM per device.

v0:
```python
import jax
import jax.numpy as jnp
from jax import lax
from jax.sharding import PartitionSpec as P


def carried_in(shard, axis, combine, identity, reverse):
    length, place = (lax.axis_size(axis), lax.axis_index(axis))
    everything = jax.tree.map(lambda part: lax.all_gather(part, axis), shard)
    start = jax.tree.map(
        lambda part, zero: jnp.broadcast_to(jnp.asarray(zero, part.dtype), part.shape),
        shard,
        identity,
    )

    def lap(k, before):
        at = length - 1 - k if reverse else k
        reached = at > place if reverse else at < place
        new = combine(before, jax.tree.map(lambda part: part[at], everything))
        return jax.tree.map(lambda a, b: jnp.where(reached, a, b), new, before)

    return lax.fori_loop(0, length, lap, start)


def block_forward(vals_in, raw_in, dt_bias, decay_rate, b_proj, c_proj, state_in):
    step_size = jax.nn.softplus(raw_in + dt_bias[None, :])
    running = jnp.cumsum(-step_size * decay_rate[None, :], axis=0)
    tok_count = vals_in.shape[0]
    row_ids = lax.broadcasted_iota(jnp.int32, (tok_count, tok_count), 0)
    col_ids = lax.broadcasted_iota(jnp.int32, (tok_count, tok_count), 1)
    causal = col_ids <= row_ids
    gap_sums = running.T[:, :, None] - running.T[:, None, :]
    weights = jnp.exp(jnp.where(causal[None, :, :], gap_sums, -1e30))
    scores = jnp.dot(c_proj, b_proj.T)
    scaled = vals_in * step_size[:, :, None]
    mixing = weights * scores[None, :, :]
    inner_part = jnp.einsum("hts,shp->thp", mixing, scaled)
    carried = jnp.einsum("tn,hpn->thp", c_proj, state_in) * jnp.exp(running)[:, :, None]
    outputs = inner_part + carried
    tail_decay = jnp.exp(running[-1][None, :] - running)
    local_state = jnp.einsum("thp,tn->hpn", scaled * tail_decay[:, :, None], b_proj)
    total_decay = jnp.exp(running[-1])
    state_out = total_decay[:, None, None] * state_in + local_state
    return (outputs, state_out)


def combine(earlier, later):
    return (earlier[0] * later[0], later[0][:, None, None] * earlier[1] + later[1])


def per_device(values, dt_raw, dt_bias, decay_rate, features, bc_weight, out_grad):
    tok_count = values.shape[1]
    head_count = dt_raw.shape[2]
    head_width = values.shape[2] // head_count
    state_size = bc_weight.shape[1] // 2
    inputs = features[0]
    part_sums = jnp.dot(inputs, bc_weight, preferred_element_type=jnp.float32)
    owned_proj = lax.psum_scatter(part_sums, "head", scatter_dimension=1, tiled=True)
    proj_bf = lax.all_gather(owned_proj.astype(jnp.bfloat16), "head", axis=1, tiled=True)
    proj_wide = proj_bf.astype(jnp.float32)
    b_proj = proj_wide[:, :state_size]
    c_proj = proj_wide[:, state_size:]
    vals_wide = values[0].astype(jnp.float32).reshape(tok_count, head_count, head_width)
    grads_wide = out_grad[0].astype(jnp.float32).reshape(tok_count, head_count, head_width)
    raw_steps = dt_raw[0]
    step_size = jax.nn.softplus(raw_steps + dt_bias[None, :])
    running = jnp.cumsum(-step_size * decay_rate[None, :], axis=0)
    total_decay = jnp.exp(running[-1])
    tail_decay = jnp.exp(running[-1][None, :] - running)
    local_state = jnp.einsum(
        "thp,tn->hpn", vals_wide * (step_size * tail_decay)[:, :, None], b_proj
    )
    local_grad = jnp.einsum("thp,tn->hpn", grads_wide * jnp.exp(running)[:, :, None], c_proj)
    identity = (
        jnp.ones((head_count,), jnp.float32),
        jnp.zeros((head_count, head_width, state_size), jnp.float32),
    )
    state_in = carried_in((total_decay, local_state), "ctx", combine, identity, False)[1]
    grad_exit = carried_in((total_decay, local_grad), "ctx", combine, identity, True)[1]

    def local_block(vals_in, raw_in, proj_in):
        return block_forward(
            vals_in,
            raw_in,
            dt_bias,
            decay_rate,
            proj_in[:, :state_size],
            proj_in[:, state_size:],
            state_in,
        )

    _, pullback = jax.vjp(local_block, vals_wide, raw_steps, proj_wide)
    value_grad, step_grad, proj_part = pullback((grads_wide, grad_exit))
    owned_grad = lax.psum_scatter(proj_part, "head", scatter_dimension=1, tiled=True)
    proj_round = lax.all_gather(owned_grad.astype(jnp.bfloat16), "head", axis=1, tiled=True)
    grad_features = jnp.dot(proj_round, bc_weight.T, preferred_element_type=jnp.float32).astype(
        jnp.bfloat16
    )
    grad_weight = lax.psum_scatter(
        jnp.einsum("tk,td->kd", proj_round, inputs, preferred_element_type=jnp.float32),
        ("ctx", "dp"),
        scatter_dimension=0,
        tiled=True,
    )
    grad_values = value_grad.reshape(tok_count, head_count * head_width).astype(jnp.bfloat16)
    return (grad_values[None], step_grad[None], grad_features[None], grad_weight)


def solution(mesh):
    return jax.shard_map(
        per_device,
        mesh=mesh,
        in_specs=(
            P("dp", "ctx", "head"),
            P("dp", "ctx", "head"),
            P("head"),
            P("head"),
            P("dp", "ctx", "head"),
            P("head", None),
            P("dp", "ctx", "head"),
        ),
        out_specs=(
            P("dp", "ctx", "head"),
            P("dp", "ctx", "head"),
            P("dp", "ctx", "head"),
            P(("ctx", "dp"), "head"),
        ),
        check_vma=False,
    )
```

profile of v0, /device:TPU:1, one launch (start us, length us, event | category | flops | bytes accessed | tf_op | source)
XLA Modules:
  0.0 1011.9 jit_solution(15322718016487212609)
XLA Ops:
  8.4 2.2 fusion.11
  13.8 28.9 %reduce-scatter.5.cloned.1.call-done = f32[128,64]{0,1:T(8,128)} async-done(((f32[128,256]{0,1:T(8,128)}), f32[128,64]{0,1:T(8,128)}) %reduce-scatter.5.cloned.1.call-update) | async-done | bytes 32784 | tf_op jit(solution)/shard_map/reduce_scatter | solution.py:58
  43.4 9.0 all_gather.24
  55.7 1.4 copy.93
  57.8 1.3 dynamic-slice
  59.8 73.1 %all-gather.2 = f32[64,1,16]{2,1,0:T(1,128)} all-gather(f32[1,1,16]{2,1,0:T(1,128)} %bitcast.111), channel_id=1, replica_groups=mesh['ctx'=64,'head'=4,'dp'=2] {'ctx'}, dimensions={0}, use_global_device_ids=true | all-gather | bytes 4160 | tf_op jit(solution)/shard_map/all_gather | solution.py:9
  133.7 2.3 fusion.7
  136.0 118.0 %all-gather.6.cloned.1.call-done = f32[1024,64,128]{2,1,0:T(8,128)} async-done(((f32[16,64,128]{2,1,0:T(8,128)}), f32[1024,64,128]{2,1,0:T(8,128)}) %all-gather.6.cloned.1.call-update) | async-done | bytes 33554448 | tf_op jit(solution)/shard_map/all_gather | solution.py:9
  254.0 153.5 %while.30 = (s32[]{:T(128)}, f32[16,64,128]{2,1,0:T(8,128)S(1)}, s32[]{:T(128)}, f32[64,16]{1,0:T(8,128)}, f32[64,16,64,128]{3,2,1,0:T(8,128)}, /*index=5*/s32[]{:T(128)}, s32[]{:T(128)}, s32[]{:T(128)}, s32[]{:T(128)}) while((s32[]{:T(128)}, f32[16,64,128]{2,1,0:T(8,128)S(1)}, s32[]{:T(128)}, f32[64,16]{1,0:T(8,128)}, ...), condition=%wide.region_3.4_spmd.clone, body=%wide.region_2.3_spmd.clone.sunk | while | flops 524296 | bytes 1573223 | solution.py:22
  276.6 1.2 fusion.65
  292.1 1.2 dynamic-slice_bitcast_fusion.4
  296.9 1.2 dynamic-slice_bitcast_fusion.4
  300.6 1.2 fusion.65
  317.4 1.2 fusion.65
  334.2 1.2 fusion.65
  349.9 1.2 dynamic-slice_bitcast_fusion.4
  351.1 1.2 fusion.65
  352.3 1.2 dynamic-slice_bitcast_fusion.4
  354.7 1.2 dynamic-slice_bitcast_fusion.4
  357.1 1.2 dynamic-slice_bitcast_fusion.4
  359.5 1.2 dynamic-slice_bitcast_fusion.4
  361.9 1.2 dynamic-slice_bitcast_fusion.4
  367.9 1.2 fusion.65
  388.3 1.2 dynamic-slice_bitcast_fusion.4
  390.7 1.2 dynamic-slice_bitcast_fusion.4
  391.9 1.2 fusion.65
  393.1 1.2 dynamic-slice_bitcast_fusion.4
  395.5 1.2 dynamic-slice_bitcast_fusion.4
  397.9 1.2 dynamic-slice_bitcast_fusion.4
  400.3 1.2 dynamic-slice_bitcast_fusion.4
  402.8 1.2 dynamic-slice_bitcast_fusion.4
  405.2 1.2 dynamic-slice_bitcast_fusion.4
  407.6 43.9 %all-gather.8.cloned.1.call-done = f32[1024,64,128]{2,1,0:T(8,128)} async-done(((f32[16,64,128]{2,1,0:T(8,128)}), f32[1024,64,128]{2,1,0:T(8,128)}) %all-gather.8.cloned.1.call-update) | async-done | bytes 33554448 | tf_op jit(solution)/shard_map/all_gather | solution.py:9
  451.5 152.4 %while.31 = (s32[]{:T(128)}, f32[16,64,128]{2,1,0:T(8,128)S(1)}, s32[]{:T(128)}, f32[64,16]{1,0:T(8,128)}, f32[64,16,64,128]{3,2,1,0:T(8,128)}, /*index=5*/s32[]{:T(128)}, s32[]{:T(128)}) while((s32[]{:T(128)}, f32[16,64,128]{2,1,0:T(8,128)S(1)}, s32[]{:T(128)}, f32[64,16]{1,0:T(8,128)}, f32[64,16,64,128]{3,2,1,0:T(8,128)}, ...), condition=%wide.region_6.7_spmd.clone, body=%wide.region_5.6_spmd.clone.sunk | while | flops 524292 | bytes 1573161 | solution.py:22
  453.9 1.2 dynamic-slice_bitcast_fusion.5
  456.3 1.2 dynamic-slice_bitcast_fusion.5
  458.7 1.2 dynamic-slice_bitcast_fusion.5
  461.1 1.2 dynamic-slice_bitcast_fusion.5
  463.5 1.2 dynamic-slice_bitcast_fusion.5
  465.8 1.2 dynamic-slice_bitcast_fusion.5
  468.2 1.2 dynamic-slice_bitcast_fusion.5
  610.4 1.7 multiply_reduce_fusion.1
  612.1 24.4 %reduce-scatter.7.cloned.1.call-done = f32[64,128]{1,0:T(8,128)} async-done(((f32[256,128]{1,0:T(8,128)}), f32[64,128]{1,0:T(8,128)}) %reduce-scatter.7.cloned.1.call-update) | async-done | bytes 32784
  637.3 9.0 all_gather.30
  646.2 1.7 fusion.9
  653.6 1.3 fusion.2
  654.9 349.0 %all-reduce.7.cloned.1.call-done = f32[256,2048]{1,0:T(8,128)} async-done(((f32[256,2048]{1,0:T(8,128)}), f32[256,2048]{1,0:T(8,128)}) %all-reduce.7.cloned.1.call-update) | async-done | bytes 2097168
  1003.9 1.5 constant_dynamic-slice_fusion
  (287 shorter events, 289.5 us)
Async XLA Ops:
  7.2 1.2 copy-start
  7.2 639.1 %copy-start.1 = (bf16[1,128,2048]{2,1,0:T(8,128)(2,1)S(1)}, bf16[1,128,2048]{2,1,0:T(8,128)(2,1)}, u32[]{:S(2)}) copy-start(bf16[1,128,2048]{2,1,0:T(8,128)(2,1)} %param.15) | copy-start | bytes 1572868
  7.2 35.5 %reduce-scatter.5.cloned.1.call-start = ((), (), s32[]{:S(2)}) async-start(), calls=%async_computation.2 | async-start | bytes 163840 | tf_op jit(solution)/shard_map/reduce_scatter | solution.py:58
  10.6 243.4 %all-gather.6.cloned.1.call-start = ((), (), s32[]{:S(2)}) async-start(), calls=%async_computation.3 | async-start | bytes 34078720 | tf_op jit(solution)/shard_map/all_gather | solution.py:9
  11.5 31.2 %copy-start.4 = (f32[128,16]{0,1:T(8,128)}, f32[128,16]{0,1:T(8,128)S(1)}, u32[]{:S(2)}) copy-start(f32[128,16]{0,1:T(8,128)S(1)} %get-tuple-element.314) | copy-start | bytes 24580
  13.8 41.9 %copy-start.3 = (f32[128,16]{0,1:T(8,128)}, f32[128,16]{0,1:T(8,128)S(1)}, u32[]{:S(2)}) copy-start(f32[128,16]{0,1:T(8,128)S(1)} %get-tuple-element.316) | copy-start | bytes 24580
  53.5 398.0 %all-gather.8.cloned.1.call-start = ((), (), s32[]{:S(2)}) async-start(), calls=%async_computation.4 | async-start | bytes 34078720 | tf_op jit(solution)/shard_map/all_gather | solution.py:9
  55.7 580.9 %reduce-scatter.7.cloned.1.call-start = ((), (), s32[]{:S(2)}) async-start(), calls=%async_computation.5 | async-start | bytes 163840
  57.8 593.5 %copy-start.2 = (f32[1,128,16]{2,1,0:T(8,128)S(1)}, f32[1,128,16]{2,1,0:T(8,128)}, u32[]{:S(2)}) copy-start(f32[1,128,16]{2,1,0:T(8,128)} %copy.93) | copy-start | bytes 24580
  132.9 0.6 copy-start.6
  133.1 0.6 copy-start.5
  610.3 393.6 %all-reduce.7.cloned.1.call-start = ((), (), s32[]{:S(2)}) async-start(), calls=%async_computation.6 | async-start | bytes 4194304
Sparse Core Ops, SparseCore 0:
  11.4 31.2 reduce-scatter.4
  53.6 200.3 all-gather.5
  256.2 195.2 all-gather.7
  610.4 26.0 reduce-scatter.6
  648.1 355.7 all-reduce.6
where the time goes:
time: 1020 us; the launch traced here: 1010 us
  waiting for transfers between devices  564 us (55%)
  local copies, waits for them, and re-layouts  166 us (16%)
  other arithmetic  157 us (15%)
  blocking collectives  91 us (9%)
  matrix products  16.5 us (2%)
  between operations  14.6 us (1%)
    unnamed x7, waiting for transfers between devices  373 us
    all_gather x2, waiting for transfers between devices, carried_in(): everything = jax.tree.map(lambda part: lax.all_gather(part, axis), shard)  162 us
    mul x128, local copies, waits for them, and re-layouts, combine(): later[0][:, None, None] * earlier[1] + later[1]  153 us
    select_n x128, other arithmetic, lap(): return jax.tree.map(lambda a, b: jnp.where(reached, a, b), new, before)  150 us
    all_gather x1, blocking collectives, carried_in(): everything = jax.tree.map(lambda part: lax.all_gather(part, axis), shard)  73.1 us
    reduce_scatter x1, waiting for transfers between devices, per_device(): lax.psum_scatter(part_sums, 'head', scatter_dimension=1, tiled=True)  28.9 us
  transfers between devices with their start and end apart: 5, of which 5 were waited for; matrix products, arithmetic and copies ran while one was open for 17% of the time, Pallas kernels for 0%

commit v1 on v0

v1 whole, which is shorter than its diff:
```python
import jax
import jax.numpy as jnp
from jax import lax
from jax.experimental import pallas as pl
from jax.experimental.pallas import tpu as pltpu
from jax.sharding import PartitionSpec as P

F32 = jnp.float32
BF16 = jnp.bfloat16
MESH_ID = pl.DeviceIdType.MESH
VMEM = pl.BlockSpec(memory_space=pltpu.VMEM)


def remote(src, dst, send_sem, recv_sem, where):
    return pltpu.make_async_remote_copy(
        src_ref=src, dst_ref=dst, send_sem=send_sem, recv_sem=recv_sem,
        device_id=where, device_id_type=MESH_ID,
    )


def greet(barrier, where):
    pl.semaphore_signal(barrier, inc=1, device_id=where, device_id_type=MESH_ID)


def far_first(k, nz):
    return nz // 2 + (1 - 2 * (k % 2)) * ((k + 1) // 2)


def head_sum_kernel(part_ref, out_ref, got, send, recv):
    me = lax.axis_index("head")
    nh = lax.axis_size("head")
    barrier = pltpu.get_barrier_semaphore()
    for d in range(1, nh):
        greet(barrier, {"head": (me + d) % nh})
    pl.semaphore_wait(barrier, nh - 1)
    copies = []
    for d in (2, 1, 3):
        copies.append(
            remote(part_ref, got.at[d - 1], send.at[d - 1], recv.at[d - 1], {"head": (me + d) % nh})
        )
        copies[-1].start()
    total = part_ref[...].astype(F32)
    for copy in copies:
        copy.wait_recv()
    for d in range(nh - 1):
        total = total + got[d].astype(F32)
    out_ref[...] = total.astype(BF16)
    for copy in copies:
        copy.wait_send()


def head_sum(part, which):
    nh = lax.axis_size("head")
    return pl.pallas_call(
        head_sum_kernel,
        out_shape=jax.ShapeDtypeStruct(part.shape, BF16),
        in_specs=[VMEM],
        out_specs=VMEM,
        scratch_shapes=[
            pltpu.VMEM((nh - 1,) + part.shape, BF16),
            pltpu.SemaphoreType.DMA((nh - 1,)),
            pltpu.SemaphoreType.DMA((nh - 1,)),
        ],
        compiler_params=pltpu.CompilerParams(collective_id=which, has_side_effects=True),
        name="head_sum",
    )(part)


def scan_kernel(sg, logs, out, r1, r1d, zs, zd, r2, r2d, bk, r4, p5, r5,
                s1, s1d, g1, g1d, s2, s2d, g2, g2d, s4, g4, s5, g5):
    ctx = lax.axis_index("ctx")
    nz = lax.axis_size("ctx") // 4
    z, p = ctx // 4, ctx % 4
    rows = 256 // nz
    barrier = pltpu.get_barrier_semaphore()
    for d in range(1, 4):
        greet(barrier, {"ctx": z * 4 + (p + d) % 4})

    def hello(k, _):
        greet(barrier, {"ctx": ((z + far_first(k, nz)) % nz) * 4 + p})
        return 0

    lax.fori_loop(0, nz - 1, hello, 0)
    pl.semaphore_wait(barrier, 3 + nz - 1)

    def to_plane(d):
        q = (p + d) % 4
        where = {"ctx": z * 4 + q}
        lanes = pl.ds(pl.multiple_of(q * 256, 256), 256)
        return (
            remote(sg.at[:, :, lanes], r1.at[p], s1.at[d - 1], g1.at[p], where),
            remote(logs.at[q], r1d.at[p], s1d.at[d - 1], g1d.at[p], where),
        )

    for d in (2, 3, 1):
        for copy in to_plane(d):
            copy.start()
    r1[p] = sg[:, :, pl.ds(pl.multiple_of(p * 256, 256), 256)]
    r1d[p] = logs[p]
    for d in range(1, 4):
        q = (p + d) % 4
        where = {"ctx": z * 4 + q}
        remote(r1.at[q], r1.at[q], s1.at[0], g1.at[q], where).wait_recv()
        remote(r1d.at[q], r1d.at[q], s1d.at[0], g1d.at[q], where).wait_recv()

    whole = r1d[0] + r1d[1] + r1d[2] + r1d[3]
    zd[0] = whole[:, :128]
    zd[1] = whole[:, 128:]
    for half in range(2):
        lanes = slice(128 * half, 128 * half + 128)
        decay = [jnp.exp(r1d[q][:, lanes]) for q in range(4)]
        fwd = r1[0, 0, :, lanes].astype(F32)
        for q in range(1, 4):
            fwd = fwd * decay[q] + r1[q, 0, :, lanes].astype(F32)
        bwd = r1[3, 1, :, lanes].astype(F32)
        for q in (2, 1, 0):
            bwd = bwd * decay[q] + r1[q, 1, :, lanes].astype(F32)
        for j in range(half, nz, 2):
            at = (j // 2) * rows
            zs[j, 0] = fwd[at:at + rows].astype(BF16)
            zs[j, 1] = bwd[at:at + rows].astype(BF16)

    def to_owner(k, _):
        peer = (z + far_first(k, nz)) % nz
        where = {"ctx": peer * 4 + p}
        remote(zs.at[peer], r2.at[z], s2.at[peer], g2.at[z], where).start()
        remote(zd.at[peer % 2], r2d.at[z], s2d.at[peer], g2d.at[z], where).start()
        return 0

    lax.fori_loop(0, nz - 1, to_owner, 0)
    r2[z] = zs[z]
    r2d[z] = zd[z % 2]

    def from_planes(k, _):
        peer = (z + 1 + k) % nz
        where = {"ctx": peer * 4 + p}
        remote(zs.at[peer], r2.at[peer], s2.at[peer], g2.at[peer], where).wait_recv()
        remote(zd.at[peer % 2], r2d.at[peer], s2d.at[peer], g2d.at[peer], where).wait_recv()
        return 0

    lax.fori_loop(0, nz - 1, from_planes, 0)

    carry = jnp.zeros((rows, 128), F32)
    back = jnp.zeros((rows, 128), F32)
    for k in range(nz):
        bk[k, 0] = carry.astype(BF16)
        carry = carry * jnp.exp(r2d[k]) + r2[k, 0].astype(F32)
        m = nz - 1 - k
        bk[m, 1] = back.astype(BF16)
        back = back * jnp.exp(r2d[m]) + r2[m, 1].astype(F32)

    def to_planes(k, _):
        peer = (z + far_first(k, nz)) % nz
        remote(bk.at[peer], r4.at[z], s4.at[peer], g4.at[z], {"ctx": peer * 4 + p}).start()
        return 0

    lax.fori_loop(0, nz - 1, to_planes, 0)
    r4[z] = bk[z]

    def from_owners(k, _):
        peer = (z + 1 + k) % nz
        remote(bk.at[peer], r4.at[peer], s4.at[peer], g4.at[peer], {"ctx": peer * 4 + p}).wait_recv()
        return 0

    lax.fori_loop(0, nz - 1, from_owners, 0)

    for half in range(2):
        lanes = slice(128 * half, 128 * half + 128)
        decay = [jnp.exp(r1d[q][:, lanes]) for q in range(4)]
        for j in range(half, nz, 2):
            span = slice((j // 2) * rows, (j // 2) * rows + rows)
            state = r4[j, 0].astype(F32)
            for q in range(4):
                p5[q, 0, span, lanes] = state.astype(BF16)
                if q < 3:
                    state = state * decay[q] + r1[q, 0, span, lanes].astype(F32)
            grad = r4[j, 1].astype(F32)
            for q in (3, 2, 1, 0):
                p5[q, 1, span, lanes] = grad.astype(BF16)
                if q > 0:
                    grad = grad * decay[q] + r1[q, 1, span, lanes].astype(F32)

    for d in (2, 3, 1):
        q = (p + d) % 4
        remote(p5.at[q], r5.at[p], s5.at[d - 1], g5.at[p], {"ctx": z * 4 + q}).start()
    r5[p] = p5[p]
    for d in range(1, 4):
        q = (p + d) % 4
        remote(p5.at[q], r5.at[q], s5.at[0], g5.at[q], {"ctx": z * 4 + q}).wait_recv()
    for q in range(4):
        out[:, :, 256 * q:256 * q + 256] = r5[q]

    for d in range(1, 4):
        q = (p + d) % 4
        for copy in to_plane(d):
            copy.wait_send()
        remote(p5.at[q], r5.at[p], s5.at[d - 1], g5.at[p], {"ctx": z * 4 + q}).wait_send()

    def sent(k, _):
        peer = (z + 1 + k) % nz
        where = {"ctx": peer * 4 + p}
        remote(zs.at[peer], r2.at[z], s2.at[peer], g2.at[z], where).wait_send()
        remote(zd.at[peer % 2], r2d.at[z], s2d.at[peer], g2d.at[z], where).wait_send()
        remote(bk.at[peer], r4.at[z], s4.at[peer], g4.at[z], where).wait_send()
        return 0

    lax.fori_loop(0, nz - 1, sent, 0)


def scan_exchange(sg, logs):
    nz = lax.axis_size("ctx") // 4
    rows = 256 // nz
    dma = pltpu.SemaphoreType.DMA
    return pl.pallas_call(
        scan_kernel,
        out_shape=jax.ShapeDtypeStruct(sg.shape, BF16),
        in_specs=[VMEM, VMEM],
        out_specs=VMEM,
        scratch_shapes=[
            pltpu.VMEM((4, 2, 128, 256), BF16),
            pltpu.VMEM((4, 1, 256), F32),
            pltpu.VMEM((nz, 2, rows, 128), BF16),
            pltpu.VMEM((2, 1, 128), F32),
            pltpu.VMEM((nz, 2, rows, 128), BF16),
            pltpu.VMEM((nz, 1, 128), F32),
            pltpu.VMEM((nz, 2, rows, 128), BF16),
            pltpu.VMEM((nz, 2, rows, 128), BF16),
            pltpu.VMEM((4, 2, 128, 256), BF16),
            pltpu.VMEM((4, 2, 128, 256), BF16),
            dma((3,)), dma((3,)), dma((4,)), dma((4,)),
            dma((nz,)), dma((nz,)), dma((nz,)), dma((nz,)),
            dma((nz,)), dma((nz,)), dma((3,)), dma((4,)),
        ],
        compiler_params=pltpu.CompilerParams(collective_id=2, has_side_effects=True),
        name="scan_exchange",
    )(sg, logs)


def weight_kernel(gw, out, e1, hs, e2, zs, e3, s1, g1, s2, g2, s3, g3):
    ctx, dp = lax.axis_index("ctx"), lax.axis_index("dp")
    nz = lax.axis_size("ctx") // 4
    width = gw.shape[1]
    block = gw.shape[0] // 8
    z, low, core = ctx // 4, (ctx // 2) % 2, ctx % 2
    y = dp * 2 + low
    other = {"ctx": ctx + 1 - 2 * core}

    def along_y(d):
        to = (y + d) % 4
        return {"ctx": z * 4 + (to % 2) * 2 + core, "dp": to // 2}

    def along_z(peer):
        return {"ctx": peer * 4 + low * 2 + core}

    barrier = pltpu.get_barrier_semaphore()

    def hello(k, _):
        greet(barrier, along_z((z + far_first(k, nz)) % nz))
        return 0

    lax.fori_loop(0, nz - 1, hello, 0)
    for d in (2, 1, 3):
        greet(barrier, along_y(d))
    greet(barrier, other)
    pl.semaphore_wait(barrier, nz - 1 + 3 + 1)

    first = remote(gw.at[pl.ds(pl.multiple_of((1 - core) * 4 * block, 4 * block), 4 * block)],
                   e1, s1, g1, other)
    first.start()
    first.wait_recv()
    mine = pl.multiple_of(core * 4 * block, 4 * block)

    def pair_sum(b):
        here = gw[pl.ds(pl.multiple_of(mine + b * block, block), block), :].astype(F32)
        there = e1[pl.ds(pl.multiple_of(b * block, block), block), :].astype(F32)
        return here + there

    for d in (2, 1, 3):
        b = (y + d) % 4
        hs[d - 1] = pair_sum(b).astype(BF16)
        remote(hs.at[d - 1], e2.at[d - 1], s2.at[d - 1], g2.at[d - 1], along_y(d)).start()
    total = pair_sum(y)
    for d in (1, 3, 2):
        remote(hs.at[d - 1], e2.at[d - 1], s2.at[d - 1], g2.at[d - 1], along_y(d)).wait_recv()
        total = total + e2[d - 1].astype(F32)
    for k in range(nz):
        zs[k] = total[2 * k:2 * k + 2].astype(BF16)

    def to_rows(k, _):
        peer = (z + far_first(k, nz)) % nz
        remote(zs.at[peer], e3.at[z], s3.at[peer], g3.at[z], along_z(peer)).start()
        return 0

    lax.fori_loop(0, nz - 1, to_rows, 0)
    e3[z] = zs[z]

    def from_all(k, _):
        peer = (z + 1 + k) % nz
        remote(zs.at[peer], e3.at[peer], s3.at[peer], g3.at[peer], along_z(peer)).wait_recv()
        return 0

    lax.fori_loop(0, nz - 1, from_all, 0)
    total = e3[0].astype(F32)
    for k in range(1, nz):
        total = total + e3[k].astype(F32)
    out[...] = total

    first.wait_send()
    for d in range(1, 4):
        remote(hs.at[d - 1], e2.at[d - 1], s2.at[d - 1], g2.at[d - 1], along_y(d)).wait_send()

    def sent(k, _):
        peer = (z + 1 + k) % nz
        remote(zs.at[peer], e3.at[z], s3.at[peer], g3.at[z], along_z(peer)).wait_send()
        return 0

    lax.fori_loop(0, nz - 1, sent, 0)


def weight_sum(gw):
    nz = lax.axis_size("ctx") // 4
    rows, width = gw.shape
    block = rows // 8
    dma = pltpu.SemaphoreType.DMA
    return pl.pallas_call(
        weight_kernel,
        out_shape=jax.ShapeDtypeStruct((2, width), F32),
        in_specs=[VMEM],
        out_specs=VMEM,
        scratch_shapes=[
            pltpu.VMEM((4 * block, width), BF16),
            pltpu.VMEM((3, block, width), BF16),
            pltpu.VMEM((3, block, width), BF16),
            pltpu.VMEM((nz, 2, width), BF16),
            pltpu.VMEM((nz, 2, width), BF16),
            dma, dma, dma((3,)), dma((3,)), dma((nz,)), dma((nz,)),
        ],
        compiler_params=pltpu.CompilerParams(collective_id=3, has_side_effects=True),
        name="weight_sum",
    )(gw)


def block_forward(vals_in, raw_in, dt_bias, decay_rate, b_proj, c_proj, state_in):
    step_size = jax.nn.softplus(raw_in + dt_bias[None, :])
    running = jnp.cumsum(-step_size * decay_rate[None, :], axis=0)
    tok_count = vals_in.shape[0]
    row_ids = lax.broadcasted_iota(jnp.int32, (tok_count, tok_count), 0)
    col_ids = lax.broadcasted_iota(jnp.int32, (tok_count, tok_count), 1)
    causal = col_ids <= row_ids
    gap_sums = running.T[:, :, None] - running.T[:, None, :]
    weights = jnp.exp(jnp.where(causal[None, :, :], gap_sums, -1e30))
    scores = jnp.dot(c_proj, b_proj.T)
    scaled = vals_in * step_size[:, :, None]
    mixing = weights * scores[None, :, :]
    inner_part = jnp.einsum("hts,shp->thp", mixing, scaled)
    carried = jnp.einsum("tn,hpn->thp", c_proj, state_in) * jnp.exp(running)[:, :, None]
    outputs = inner_part + carried
    tail_decay = jnp.exp(running[-1][None, :] - running)
    local_state = jnp.einsum("thp,tn->hpn", scaled * tail_decay[:, :, None], b_proj)
    total_decay = jnp.exp(running[-1])
    state_out = total_decay[:, None, None] * state_in + local_state
    return (outputs, state_out)


def per_device(values, dt_raw, dt_bias, decay_rate, features, bc_weight, out_grad):
    tok_count = values.shape[1]
    head_count = dt_raw.shape[2]
    head_width = values.shape[2] // head_count
    state_size = bc_weight.shape[1] // 2
    nz = lax.axis_size("ctx") // 4
    inputs = features[0]
    part_sums = jnp.dot(inputs, bc_weight, preferred_element_type=F32).astype(BF16)
    proj_bf = head_sum(part_sums, 0)
    proj_wide = proj_bf.astype(F32)
    b_proj = proj_bf[:, :state_size]
    c_proj = proj_bf[:, state_size:]
    vals_wide = values[0].astype(F32).reshape(tok_count, head_count, head_width)
    grads_wide = out_grad[0].astype(F32).reshape(tok_count, head_count, head_width)
    raw_steps = dt_raw[0]
    step_size = jax.nn.softplus(raw_steps + dt_bias[None, :])
    running = jnp.cumsum(-step_size * decay_rate[None, :], axis=0)
    tail_decay = jnp.exp(running[-1][None, :] - running)
    wide = head_count * head_width
    vals_in = (vals_wide * (step_size * tail_decay)[:, :, None]).astype(BF16).reshape(tok_count, wide)
    grads_in = (grads_wide * jnp.exp(running)[:, :, None]).astype(BF16).reshape(tok_count, wide)
    over_tokens = (((0,), (0,)), ((), ()))
    local = jnp.stack([
        lax.dot_general(b_proj, vals_in, over_tokens, preferred_element_type=F32).astype(BF16),
        lax.dot_general(c_proj, grads_in, over_tokens, preferred_element_type=F32).astype(BF16),
    ])
    logs = jnp.repeat(running[-1], head_width).reshape(4, 1, 256)
    carried = scan_exchange(local, logs).astype(F32)
    carried = carried.reshape(2, state_size, head_count, head_width).transpose(0, 2, 3, 1)
    state_in, grad_exit = carried[0], carried[1]

    def local_block(vals_in, raw_in, proj_in):
        return block_forward(
            vals_in, raw_in, dt_bias, decay_rate,
            proj_in[:, :state_size], proj_in[:, state_size:], state_in,
        )

    _, pullback = jax.vjp(local_block, vals_wide, raw_steps, proj_wide)
    value_grad, step_grad, proj_part = pullback((grads_wide, grad_exit))
    proj_round = head_sum(proj_part.astype(BF16), 1)
    grad_features = jnp.dot(proj_round, bc_weight.T, preferred_element_type=F32).astype(BF16)
    ordered = proj_round.reshape(tok_count, nz, 2, 2, 2, 2 * state_size // (8 * nz))
    ordered = ordered.transpose(0, 3, 4, 2, 1, 5).reshape(tok_count, 2 * state_size)
    partial = lax.dot_general(ordered, inputs, over_tokens, preferred_element_type=F32).astype(BF16)
    grad_weight = weight_sum(partial)
    grad_values = value_grad.reshape(tok_count, wide).astype(BF16)
    return (grad_values[None], step_grad[None], grad_features[None], grad_weight)


def solution(mesh):
    return jax.shard_map(
        per_device,
        mesh=mesh,
        in_specs=(
            P("dp", "ctx", "head"),
            P("dp", "ctx", "head"),
            P("head"),
            P("head"),
            P("dp", "ctx", "head"),
            P("head", None),
            P("dp", "ctx", "head"),
        ),
        out_specs=(
            P("dp", "ctx", "head"),
            P("dp", "ctx", "head"),
            P("dp", "ctx", "head"),
            P(("ctx", "dp"), "head"),
        ),
        check_vma=False,
    )
```

time: 1020 us -> 119 us (0.12)
  waiting for transfers between devices: 564 us -> 0 us
  local copies, waits for them, and re-layouts: 166 us -> 7.65 us
  other arithmetic: 157 us -> 4.65 us
  Pallas kernels: 0 us -> 95.8 us
  blocking collectives: 91 us -> 0 us
  between operations: 14.6 us -> 0.91 us
    unnamed x7 -> x0, waiting for transfers between devices: 373 us -> none
    all_gather x2 -> x0, waiting for transfers between devices: 162 us -> none  [carried_in(): everything = jax.tree.map(lambda part: lax.all_gather(part, axis), shard)]
    mul x128 -> x0, local copies, waits for them, and re-layouts: 153 us -> none  [combine(): later[0][:, None, None] * earlier[1] + later[1]]
    select_n x128 -> x0, other arithmetic: 150 us -> none  [lap(): return jax.tree.map(lambda a, b: jnp.where(reached, a, b), new, before)]
    pallas_call x0 -> x4, Pallas kernels: none -> 95.8 us  [the longest x1 48.8 us: scan_exchange(): pl.pallas_call(scan_kernel, out_shape=jax.ShapeDtypeStruct(sg.shape, BF16...]
    all_gather x3 -> x0, blocking collectives: 91 us -> none  [the longest x1 73.1 us: carried_in(): everything = jax.tree.map(lambda part: lax.all_gather(part, axis), shard)]
    reduce_scatter x1 -> x0, waiting for transfers between devices: 28.9 us -> none  [per_device(): lax.psum_scatter(part_sums, 'head', scatter_dimension=1, tiled=True)]
  transfers between devices with their start and end apart: 5 -> 0, of which waited for: 5 -> 0; matrix products, arithmetic and copies ran while one was open for 17% -> 0% of each run, Pallas kernels for 0% -> 0%
where the time goes in v1:
time: 119 us
  Pallas kernels  95.8 us (81%)
  matrix products  9.76 us (8%)
  local copies, waits for them, and re-layouts  7.65 us (6%)
  other arithmetic  4.65 us (4%)
    pallas_call x1, Pallas kernels, scan_exchange(): pl.pallas_call(scan_kernel, out_shape=jax.ShapeDtypeStruct(sg.shape, BF16...  48.8 us
    pallas_call x1, Pallas kernels, weight_sum(): pl.pallas_call(weight_kernel, out_shape=jax.ShapeDtypeStruct((2, width),...  29 us
    pallas_call x2, Pallas kernels, head_sum(): pl.pallas_call(head_sum_kernel, out_shape=jax.ShapeDtypeStruct(part.shape...  18.1 us
    unnamed x22, local copies, waits for them, and re-layouts  3.71 us

profile of v1, /device:TPU:1, one launch (start us, length us, event | category | flops | bytes accessed | tf_op | source)
XLA Modules:
  0.0 118.8 jit_solution(6643981402834377561)
XLA Ops:
  0.7 0.9 negate_multiply_fusion
  1.6 0.1 copy.91
  1.7 0.2 reduce_window_sum.26
  1.9 0.2 slice_reduce_fusion
  2.1 0.1 broadcast_in_dim.26
  2.3 0.7 broadcast_in_dim.28.logs
  3.1 0.8 copy.106
  3.9 2.0 %convolution_convert_fusion.4.part_ref = bf16[128,256]{1,0:T(8,128)(2,1)} fusion(bf16[2048,256]{1,0:T(8,128)(2,1)S(1)} %copy-done, bf16[1,128,2048]{2,1,0:T(8,128)(2,1)} %param.11), kind=kOutput, calls=%fused_computation.12 | convolution fusion | flops 134250496 | bytes 1638400 | tf_op jit(solution)/shard_map/dot_general | solution.py:372
  5.9 9.0 %head_sum.2 = bf16[128,256]{1,0:T(8,128)(2,1)} custom-call(bf16[128,256]{1,0:T(8,128)(2,1)} %convolution_convert_fusion.4.part_ref), custom_call_target="tpu_custom_call" | custom-call | tf_op jit(solution)/shard_map/head_sum/pallas_call | solution.py:54
  15.0 0.9 fusion.29
  15.9 0.2 copy.94
  16.1 0.2 copy.90
  16.3 0.1 fusion.9
  16.4 0.4 copy-done.2
  16.7 0.2 fusion.4
  17.0 0.2 fusion.3
  17.2 0.8 pad_maximum_fusion.sg
  18.1 48.8 %scan_exchange.1 = bf16[2,128,1024]{2,1,0:T(8,128)(2,1)} custom-call(bf16[2,128,1024]{2,1,0:T(8,128)(2,1)} %pad_maximum_fusion.sg, f32[4,1,256]{2,1,0:T(1,128)} %broadcast_in_dim.28.logs), custom_call_target="tpu_custom_call" | custom-call | tf_op jit(solution)/shard_map/scan_exchange/pallas_call | solution.py:214
  66.9 1.3 %copy.96 = bf16[2,128,1024]{1,2,0:T(8,128)(2,1)S(1)} copy(bf16[2,128,1024]{2,1,0:T(8,128)(2,1)} %scan_exchange.1) | data formatting | bytes 1048576 | tf_op jit(solution)/shard_map/scan_exchange/pallas_call | solution.py:214
  68.2 0.2 fusion.2
  68.4 0.1 convert_multiply_fusion
  68.6 0.3 convolution_bitcast_fusion.3
  68.8 0.3 convolution_bitcast_fusion.2
  69.1 0.2 fusion.21
  69.3 0.6 multiply_reduce_fusion.1
  69.9 0.9 fusion.7
  70.8 0.1 convolution_add_fusion
  71.0 0.2 convolution_add_fusion.1
  71.2 0.6 add_convert_fusion.part_ref
  71.8 9.1 %head_sum.3 = bf16[128,256]{1,0:T(8,128)(2,1)} custom-call(bf16[128,256]{1,0:T(8,128)(2,1)} %add_convert_fusion.part_ref), custom_call_target="tpu_custom_call" | custom-call | tf_op jit(solution)/shard_map/head_sum/pallas_call | solution.py:54
  80.9 0.1 multiply_reduce_fusion.3
  81.0 0.1 copy.104
  81.1 0.1 copy.102
  81.2 1.0 copy.107
  82.2 0.9 copy.109
  83.1 2.1 %fusion = bf16[1,128,2048]{2,1,0:T(8,128)(2,1)} fusion(bf16[128,256]{1,0:T(8,128)(2,1)} %head_sum.3, bf16[2048,256]{1,0:T(8,128)(2,1)S(1)} %copy-done), kind=kOutput, calls=%fused_computation.2 | convolution fusion | flops 134479872 | bytes 1638400 | tf_op jit(solution)/shard_map/dot_general | solution.py:405
  85.2 1.4 %convolution_convert_fusion.gw = bf16[256,2048]{1,0:T(8,128)(2,1)} fusion(bf16[128,256]{0,1:T(8,128)(2,1)S(1)} %bitcast.116, bf16[1,128,2048]{2,1,0:T(8,128)(2,1)S(1)} %copy-done.1), kind=kOutput, calls=%fused_computation | convolution fusion | flops 134742016 | bytes 1638400 | tf_op jit(solution)/shard_map/dot_general | solution.py:408
  86.6 29.0 %weight_sum.1 = f32[2,2048]{1,0:T(2,128)} custom-call(bf16[256,2048]{1,0:T(8,128)(2,1)} %convolution_convert_fusion.gw), custom_call_target="tpu_custom_call" | custom-call | tf_op jit(solution)/shard_map/weight_sum/pallas_call | solution.py:325
  115.6 0.1 bitcast_convert_fusion
  115.7 0.2 fusion.10
  115.9 0.1 copy.103
  116.0 0.1 exponential_multiply_fusion
  116.1 0.1 fusion.36
  116.2 0.1 copy.105
  116.3 1.1 reduce_window_sum.28
  117.4 0.1 fusion.24
  117.5 0.7 copy.110
  118.2 0.6 copy.114
  (21 shorter events, 0.4 us)
Async XLA Ops:
  0.6 3.3 %copy-start = (bf16[2048,256]{1,0:T(8,128)(2,1)S(1)}, bf16[2048,256]{1,0:T(8,128)(2,1)}, u32[]{:S(2)}) copy-start(bf16[2048,256]{1,0:T(8,128)(2,1)} %param.12) | copy-start | bytes 3145732
  3.0 12.9 %copy-start.3 = (bf16[1,128,1024]{2,1,0:T(8,128)(2,1)S(1)}, bf16[1,128,1024]{2,1,0:T(8,128)(2,1)}, u32[]{:S(2)}) copy-start(bf16[1,128,1024]{2,1,0:T(8,128)(2,1)} %param.13) | copy-start | bytes 786436
  3.9 12.2 %copy-start.4 = (bf16[1,128,1024]{2,1,0:T(8,128)(2,1)S(1)}, bf16[1,128,1024]{2,1,0:T(8,128)(2,1)}, u32[]{:S(2)}) copy-start(bf16[1,128,1024]{2,1,0:T(8,128)(2,1)} %param.7) | copy-start | bytes 786436
  15.9 0.9 copy-start.2
  82.2 3.0 %copy-start.1 = (bf16[1,128,2048]{2,1,0:T(8,128)(2,1)S(1)}, bf16[1,128,2048]{2,1,0:T(8,128)(2,1)}, u32[]{:S(2)}) copy-start(bf16[1,128,2048]{2,1,0:T(8,128)(2,1)} %param.11) | copy-start | bytes 1572868
  115.7 1.7 %copy-start.6 = (f32[16]{0:T(128)S(1)}, f32[16]{0:T(128)}, u32[]{:S(2)}) copy-start(f32[16]{0:T(128)} %param.10) | copy-start | bytes 196
  115.7 1.7 %copy-start.7 = (f32[16]{0:T(128)S(1)}, f32[16]{0:T(128)}, u32[]{:S(2)}) copy-start(f32[16]{0:T(128)} %param.9) | copy-start | bytes 196
  115.7 2.5 %copy-start.5 = (f32[2,2048]{1,0:T(2,128)S(1)}, f32[2,2048]{1,0:T(2,128)}, u32[]{:S(2)}) copy-start(f32[2,2048]{1,0:T(2,128)} %weight_sum.1) | copy-start | bytes 49156

commit v2 on v0

v2 whole, which is shorter than its diff:
```python
import jax
import jax.numpy as jnp
from jax import lax
from jax.experimental import pallas as pl
from jax.experimental.pallas import tpu as pltpu
from jax.sharding import PartitionSpec as P

F32 = jnp.float32
BF16 = jnp.bfloat16
EXACT = lax.Precision.HIGHEST
MESH_ID = pl.DeviceIdType.MESH
VMEM = pl.BlockSpec(memory_space=pltpu.VMEM)
DMA = pltpu.SemaphoreType.DMA


def remote(src, dst, send_sem, recv_sem, where):
    return pltpu.make_async_remote_copy(
        src_ref=src, dst_ref=dst, send_sem=send_sem, recv_sem=recv_sem,
        device_id=where, device_id_type=MESH_ID,
    )


def greet(barrier, where):
    pl.semaphore_signal(barrier, inc=1, device_id=where, device_id_type=MESH_ID)


def far_first(k, nz):
    return nz // 2 + (1 - 2 * (k % 2)) * ((k + 1) // 2)


def dot(a, b, ca, cb, precision=None):
    return lax.dot_general(
        a, b, (((ca,), (cb,)), ((), ())), precision=precision, preferred_element_type=F32
    )


def iota(shape, dim):
    return lax.broadcasted_iota(jnp.int32, shape, dim)


def scratch_plan(nz, tokens, heads, feats, two_n):
    rows = 256 // nz
    half = feats // 2
    block = two_n // 8
    wide = heads * 64
    return dict(
        ha=pltpu.VMEM((tokens, two_n), BF16),
        hb=pltpu.VMEM((tokens, two_n), BF16),
        ga=pltpu.VMEM((3, tokens, two_n), BF16),
        gb=pltpu.VMEM((3, tokens, two_n), BF16),
        ha_s=DMA((3,)), ha_r=DMA((3,)), hb_s=DMA((3,)), hb_r=DMA((3,)),
        lg=pltpu.VMEM((4, 1, 256), F32),
        ld=pltpu.VMEM((4, 1, 256), F32),
        zl=pltpu.VMEM((2, 1, 128), F32),
        zd=pltpu.VMEM((nz, 1, 128), F32),
        lg_s=DMA((3,)), lg_r=DMA((4,)), zl_s=DMA((nz,)), zl_r=DMA((nz,)),
        vin=pltpu.VMEM((tokens, wide), BF16),
        gin=pltpu.VMEM((tokens, wide), BF16),
        sg=pltpu.VMEM((2, 128, wide), BF16),
        r1=pltpu.VMEM((2, 4, 128, 256), BF16),
        zs=pltpu.VMEM((2, nz, rows, 128), BF16),
        r2=pltpu.VMEM((2, nz, rows, 128), BF16),
        bk=pltpu.VMEM((2, nz, rows, 128), BF16),
        r4=pltpu.VMEM((2, nz, rows, 128), BF16),
        p5=pltpu.VMEM((2, 4, 128, 256), BF16),
        r5=pltpu.VMEM((2, 4, 128, 256), BF16),
        s1=DMA((2, 3)), g1=DMA((2, 4)), s2=DMA((2, nz)), g2=DMA((2, nz)),
        s4=DMA((2, nz)), g4=DMA((2, nz)), s5=DMA((2, 3)), g5=DMA((2, 4)),
        dx=pltpu.VMEM((tokens, wide), F32),
        drow=pltpu.VMEM((tokens, tokens), F32),
        pt=pltpu.VMEM((two_n, tokens), BF16),
        w0=pltpu.VMEM((2, two_n // 2, half), BF16),
        w1=pltpu.VMEM((2, two_n // 2, half), F32),
        e1=pltpu.VMEM((2, two_n // 2, half), BF16),
        hs=pltpu.VMEM((2, 3, block, half), BF16),
        e2=pltpu.VMEM((2, 3, block, half), BF16),
        ws=pltpu.VMEM((2, nz, 2, half), BF16),
        e3=pltpu.VMEM((2, nz, 2, half), BF16),
        a1=DMA((2,)), b1=DMA((2,)), a2=DMA((2, 3)), b2=DMA((2, 3)),
        a3=DMA((2, nz)), b3=DMA((2, nz)),
    )


def make_kernel(names):
    def kernel(values, raw, bias, rate, features, weight, out_grad,
               grad_values, grad_dt, grad_features, grad_weight, *scratch):
        s = dict(zip(names, scratch))
        step(values, raw, bias, rate, features, weight, out_grad,
             grad_values, grad_dt, grad_features, grad_weight, **s)
    return kernel


def step(values, raw, bias, rate, features, weight, out_grad,
         grad_values, grad_dt, grad_features, grad_weight, *,
         ha, hb, ga, gb, ha_s, ha_r, hb_s, hb_r,
         lg, ld, zl, zd, lg_s, lg_r, zl_s, zl_r,
         vin, gin, sg, r1, zs, r2, bk, r4, p5, r5, s1, g1, s2, g2, s4, g4, s5, g5,
         dx, drow, pt, w0, w1, e1, hs, e2, ws, e3, a1, b1, a2, b2, a3, b3):
    ctx, head, dp = lax.axis_index("ctx"), lax.axis_index("head"), lax.axis_index("dp")
    nz = zd.shape[0]
    z, p = ctx // 4, ctx % 4
    low, core = (ctx // 2) % 2, ctx % 2
    y = dp * 2 + low
    rows = 256 // nz
    tokens, heads = raw.shape
    pairs = heads // 2
    state = 128
    half = features.shape[1] // 2
    block = weight.shape[1] // 8

    def at_head(d):
        return {"head": (head + d) % 4}

    def in_plane(d):
        return {"ctx": z * 4 + (p + d) % 4}

    def along_z(peer):
        return {"ctx": peer * 4 + p}

    def along_y(d):
        to = (y + d) % 4
        return {"ctx": z * 4 + (to % 2) * 2 + core, "dp": to // 2}

    other = {"ctx": ctx + 1 - 2 * core}

    barrier = pltpu.get_barrier_semaphore()

    def hello(k, _):
        greet(barrier, along_z((z + far_first(k, nz)) % nz))
        return 0

    lax.fori_loop(0, nz - 1, hello, 0)
    for d in (2, 1, 3):
        greet(barrier, along_y(d))
        greet(barrier, at_head(d))
        greet(barrier, in_plane(d))

    ha[...] = dot(features[...], weight[...], 1, 0).astype(BF16)

    pre = raw[...] + bias[...]
    dt = jax.nn.softplus(pre)
    lower = (iota((tokens, tokens), 0) >= iota((tokens, tokens), 1)).astype(F32)
    run = dot(lower, -dt * rate[...], 1, 0, EXACT)
    last = run[tokens - 1:tokens, :]
    into = jnp.exp(run)
    tail = jnp.exp(last - run)
    ends = jnp.exp(last)
    run_t = jnp.concatenate([run, jnp.zeros((tokens, 128 - heads), F32)], axis=1).T
    first_half = iota((tokens, 128), 1) < 64

    def spread(cols, j):
        return jnp.where(first_half, cols[:, 2 * j:2 * j + 1], cols[:, 2 * j + 1:2 * j + 2])

    row_half = iota((1, 128), 1) < 64
    for j in range(pairs):
        lg[j // 2, :, 128 * (j % 2):128 * (j % 2) + 128] = jnp.where(
            row_half, last[:, 2 * j:2 * j + 1], last[:, 2 * j + 1:2 * j + 2]
        )
    dt_tail = dt * tail
    for j in range(pairs):
        lanes = slice(128 * j, 128 * j + 128)
        vin[:, lanes] = (values[:, lanes].astype(F32) * spread(dt_tail, j)).astype(BF16)
        gin[:, lanes] = (out_grad[:, lanes].astype(F32) * spread(into, j)).astype(BF16)

    pl.semaphore_wait(barrier, nz - 1 + 9)

    def head_copy(src, dst, ss, rs, d):
        return remote(src, dst.at[d - 1], ss.at[d - 1], rs.at[d - 1], at_head(d))

    for d in (2, 1, 3):
        head_copy(ha, ga, ha_s, ha_r, d).start()
    for d in (2, 3, 1):
        q = (p + d) % 4
        remote(lg.at[q], ld.at[p], lg_s.at[d - 1], lg_r.at[p], in_plane(d)).start()
    ld[p] = lg[p]
    for d in (1, 2, 3):
        q = (p + d) % 4
        remote(lg.at[q], ld.at[q], lg_s.at[d - 1], lg_r.at[q], in_plane(d)).wait_recv()
    whole = ld[0] + ld[1] + ld[2] + ld[3]
    zl[0] = whole[:, :128]
    zl[1] = whole[:, 128:]

    def send_decay(k, _):
        peer = (z + far_first(k, nz)) % nz
        remote(zl.at[peer % 2], zd.at[z], zl_s.at[peer], zl_r.at[z], along_z(peer)).start()
        return 0

    lax.fori_loop(0, nz - 1, send_decay, 0)
    zd[z] = zl[z % 2]

    total = ha[...].astype(F32)
    for d in (1, 3, 2):
        head_copy(ha, ga, ha_s, ha_r, d).wait_recv()
        total = total + ga[d - 1].astype(F32)
    proj = total.astype(BF16)
    b_proj = proj[:, :state]
    c_proj = proj[:, state:]
    proj_wide = proj.astype(F32)
    b_flip = proj_wide[:, :state].T.astype(BF16)
    c_flip = proj_wide[:, state:].T.astype(BF16)

    def plane_copy(src, dst, ss, rs, w, d):
        q = (p + d) % 4
        lanes = pl.ds(pl.multiple_of(q * 256, 256), 256)
        return remote(src.at[w, :, lanes], dst.at[w, p], ss.at[w, d - 1], rs.at[w, p], in_plane(d))

    for w, flip, fed in ((0, b_flip, vin), (1, c_flip, gin)):
        sg[w] = dot(flip, fed[...], 1, 0).astype(BF16)
        for d in (2, 3, 1):
            plane_copy(sg, r1, s1, g1, w, d).start()
        r1[w, p] = sg[w, :, pl.ds(pl.multiple_of(p * 256, 256), 256)]

    def plane_wait(buf, rs, ss, w):
        for d in (1, 3, 2):
            q = (p + d) % 4
            remote(buf.at[w, q], buf.at[w, q], ss.at[w, d - 1], rs.at[w, q], in_plane(d)).wait_recv()

    decays = [jnp.exp(ld[q]) for q in range(4)]

    def combine(w):
        order = (0, 1, 2, 3) if w == 0 else (3, 2, 1, 0)
        for side in range(2):
            lanes = slice(128 * side, 128 * side + 128)
            acc = r1[w, order[0], :, lanes].astype(F32)
            for n, q in enumerate(order[1:]):
                by = decays[q][:, lanes]
                acc = acc * by + r1[w, q, :, lanes].astype(F32)
            for j in range(side, nz, 2):
                at = (j // 2) * rows
                zs[w, j] = acc[at:at + rows].astype(BF16)

    def z_send(src, dst, ss, rs, w):
        def go(k, _):
            peer = (z + far_first(k, nz)) % nz
            remote(src.at[w, peer], dst.at[w, z], ss.at[w, peer], rs.at[w, z], along_z(peer)).start()
            return 0

        lax.fori_loop(0, nz - 1, go, 0)
        dst[w, z] = src[w, z]

    def z_wait(src, dst, ss, rs, w):
        def go(k, _):
            peer = (z + 1 + k) % nz
            remote(src.at[w, peer], dst.at[w, peer], ss.at[w, peer], rs.at[w, peer],
                   along_z(peer)).wait_recv()
            return 0

        lax.fori_loop(0, nz - 1, go, 0)

    for w in range(2):
        plane_wait(r1, g1, s1, w)
        combine(w)
        z_send(zs, r2, s2, g2, w)

    scores_t = dot(b_proj, c_proj, 1, 1)
    causal_t = iota((tokens, tokens), 0) <= iota((tokens, tokens), 1)
    strict_t = iota((tokens, tokens), 0) < iota((tokens, tokens), 1)
    strict_scores = jnp.where(strict_t, scores_t, 0.0)
    lane = iota((tokens, heads), 1)
    drow[...] = jnp.zeros_like(drow)

    def local_pairs(lo, hi, dscore, dcol):
        for j in range(lo, hi):
            lanes = slice(128 * j, 128 * j + 128)
            grads = out_grad[:, lanes]
            zero = jnp.zeros_like(grads)
            split = jnp.concatenate(
                [jnp.where(first_half, grads, zero), jnp.where(first_half, zero, grads)], axis=0
            )
            products = dot(values[:, lanes], split, 1, 1)
            mixes = []
            for i in range(2):
                h = 2 * j + i
                gap = run_t[h:h + 1, :] - run[:, h:h + 1]
                fall = jnp.exp(jnp.where(causal_t, gap, -1e30))
                mixes.append((fall * scores_t).astype(BF16))
                part = fall * (products[:, 128 * i:128 * i + 128] * dt[:, h:h + 1])
                dscore = dscore + part
                part = part * strict_scores
                drow[h:h + 1, :] = jnp.sum(part, axis=0, keepdims=True)
                dcol = jnp.where(lane == h, jnp.sum(part, axis=1, keepdims=True), dcol)
            dx[:, lanes] = dot(jnp.concatenate(mixes, axis=1), split, 1, 0)
        return dscore, dcol

    dscore = jnp.zeros((tokens, tokens), F32)
    dcol = jnp.zeros((tokens, heads), F32)
    dscore, dcol = local_pairs(0, pairs // 2, dscore, dcol)

    z_decays = None

    def owner_scan(w):
        carry = jnp.zeros((rows, 128), F32)
        for k in range(nz):
            m = k if w == 0 else nz - 1 - k
            bk[w, m] = carry.astype(BF16)
            carry = carry * jnp.exp(zd[m]) + r2[w, m].astype(F32)

    def decay_wait(k, _):
        peer = (z + 1 + k) % nz
        remote(zl.at[peer % 2], zd.at[peer], zl_s.at[peer], zl_r.at[peer], along_z(peer)).wait_recv()
        return 0

    lax.fori_loop(0, nz - 1, decay_wait, 0)
    for w in range(2):
        z_wait(zs, r2, s2, g2, w)
        owner_scan(w)
        z_send(bk, r4, s4, g4, w)

    dscore, dcol = local_pairs(pairs // 2, pairs, dscore, dcol)
    dscore_t = dscore.astype(BF16)
    dscore_n = dscore.T.astype(BF16)
    grad_b = dot(dscore_t, c_proj, 1, 0)
    grad_c = dot(dscore_n, b_proj, 1, 0)
    dr = drow[...].T[:, :heads] - dcol

    def expand(w):
        order = (0, 1, 2, 3) if w == 0 else (3, 2, 1, 0)
        for j in range(nz):
            span = slice((j // 2) * rows, (j // 2) * rows + rows)
            lanes = slice(128 * (j % 2), 128 * (j % 2) + 128)
            carry = r4[w, j].astype(F32)
            for n, q in enumerate(order):
                p5[w, q, span, lanes] = carry.astype(BF16)
                if n < 3:
                    carry = carry * decays[q][:, lanes] + r1[w, q, span, lanes].astype(F32)

    def back_copy(w, d):
        q = (p + d) % 4
        return remote(p5.at[w, q], r5.at[w, p], s5.at[w, d - 1], g5.at[w, p], in_plane(d))

    for w in range(2):
        z_wait(bk, r4, s4, g4, w)
        expand(w)
        for d in (2, 3, 1):
            back_copy(w, d).start()
        r5[w, p] = p5[w, p]

    group = (iota((256, 128), 0) // 64) == iota((256, 128), 1)
    groups = group.astype(F32)

    def head_sums(wide_rows):
        return dot(wide_rows, groups, 1, 0, EXACT)[:, :4]

    plane_wait(r5, g5, s5, 0)
    gains = []
    for q in range(4):
        lanes = slice(256 * q, 256 * q + 256)
        states = r5[0, q]
        grads = gin[:, lanes]
        gains.append(head_sums(dot(c_proj, states, 1, 0) * grads.astype(F32)))
        grad_c = grad_c + dot(grads, states, 1, 1)
    dr = dr + jnp.concatenate(gains, axis=1)

    plane_wait(r5, g5, s5, 1)
    falls, value_dots, kept = [], [], []
    for q in range(4):
        lanes = slice(256 * q, 256 * q + 256)
        exits = r5[1, q]
        fed = vin[:, lanes]
        reach = dot(b_proj, exits, 1, 0)
        falls.append(head_sums(reach * fed.astype(F32)))
        grad_b = grad_b + dot(fed, exits, 1, 1)
        wide_tail = jnp.concatenate([spread(tail, 2 * q), spread(tail, 2 * q + 1)], axis=1)
        full = dx[:, lanes] + reach * wide_tail
        dx[:, lanes] = full
        kept.append(head_sums(jnp.sum(
            exits.astype(F32) * r5[0, q].astype(F32), axis=0, keepdims=True
        )))
    hb[:, :state] = grad_b.astype(BF16)
    hb[:, state:] = grad_c.astype(BF16)
    for d in (2, 1, 3):
        head_copy(hb, gb, hb_s, hb_r, d).start()

    for q in range(4):
        lanes = slice(256 * q, 256 * q + 256)
        full = dx[:, lanes]
        value_dots.append(head_sums(full * values[:, lanes].astype(F32)))
        wide_dt = jnp.concatenate([spread(dt, 2 * q), spread(dt, 2 * q + 1)], axis=1)
        grad_values[:, lanes] = (full * wide_dt).astype(BF16)
    fall = jnp.concatenate(falls, axis=1)
    dr = dr - fall
    at_end = jnp.sum(fall, axis=0, keepdims=True) + ends * jnp.concatenate(kept, axis=1)
    upper = (iota((tokens, tokens), 0) <= iota((tokens, tokens), 1)).astype(F32)
    dlog = dot(upper, dr, 1, 0, EXACT) + at_end
    grad_dt[...] = (jnp.concatenate(value_dots, axis=1) - rate[...] * dlog) * jax.nn.sigmoid(pre)

    total = hb[...].astype(F32)
    for d in (1, 3, 2):
        head_copy(hb, gb, hb_s, hb_r, d).wait_recv()
        total = total + gb[d - 1].astype(F32)
    rounded = total.astype(BF16)

    new_row = iota((2 * state, 2 * state), 0)
    inner = 2 * state // (8 * nz)
    old_row = (
        ((new_row // inner) % nz) * (8 * inner)
        + ((new_row // (inner * nz)) % 2) * (4 * inner)
        + (new_row // (4 * inner * nz)) * (2 * inner)
        + ((new_row // (2 * inner * nz)) % 2) * inner
        + new_row % inner
    )
    pick = (iota((2 * state, 2 * state), 1) == old_row).astype(BF16)
    pt[...] = dot(pick, rounded, 1, 1).astype(BF16)
    there = pt[pl.ds(pl.multiple_of((1 - core) * state, state), state), :]
    here = pt[pl.ds(pl.multiple_of(core * state, state), state), :]

    def pair_copy(c):
        return remote(w0.at[c], e1.at[c], a1.at[c], b1.at[c], other)

    def y_copy(c, d):
        return remote(hs.at[c, d - 1], e2.at[c, d - 1], a2.at[c, d - 1], b2.at[c, d - 1], along_y(d))

    for c in range(2):
        w0[c] = dot(there, features[:, half * c:half * c + half], 1, 0).astype(BF16)
        pair_copy(c).start()
    for c in range(2):
        w1[c] = dot(here, features[:, half * c:half * c + half], 1, 0)
    for c in range(2):
        pair_copy(c).wait_recv()
        for d in (2, 1, 3):
            span = pl.ds(pl.multiple_of(((y + d) % 4) * block, block), block)
            hs[c, d - 1] = (w1[c, span, :] + e1[c, span, :].astype(F32)).astype(BF16)
            y_copy(c, d).start()

    grad_features[...] = dot(rounded, weight[...], 1, 1).astype(BF16)

    for c in range(2):
        span = pl.ds(pl.multiple_of(y * block, block), block)
        total = w1[c, span, :] + e1[c, span, :].astype(F32)
        for d in (1, 3, 2):
            y_copy(c, d).wait_recv()
            total = total + e2[c, d - 1].astype(F32)
        for k in range(nz):
            ws[c, k] = total[2 * k:2 * k + 2].astype(BF16)
        z_send(ws, e3, a3, b3, c)
    for c in range(2):
        z_wait(ws, e3, a3, b3, c)
        total = e3[c, 0].astype(F32)
        for k in range(1, nz):
            total = total + e3[c, k].astype(F32)
        grad_weight[:, half * c:half * c + half] = total

    for d in (1, 2, 3):
        q = (p + d) % 4
        head_copy(ha, ga, ha_s, ha_r, d).wait_send()
        head_copy(hb, gb, hb_s, hb_r, d).wait_send()
        remote(lg.at[q], ld.at[p], lg_s.at[d - 1], lg_r.at[p], in_plane(d)).wait_send()
        for w in range(2):
            plane_copy(sg, r1, s1, g1, w, d).wait_send()
            back_copy(w, d).wait_send()
            y_copy(w, d).wait_send()
    for c in range(2):
        pair_copy(c).wait_send()

    def sent(k, _):
        peer = (z + 1 + k) % nz
        where = along_z(peer)
        remote(zl.at[peer % 2], zd.at[z], zl_s.at[peer], zl_r.at[z], where).wait_send()
        for w in range(2):
            remote(zs.at[w, peer], r2.at[w, z], s2.at[w, peer], g2.at[w, z], where).wait_send()
            remote(bk.at[w, peer], r4.at[w, z], s4.at[w, peer], g4.at[w, z], where).wait_send()
            remote(ws.at[w, peer], e3.at[w, z], a3.at[w, peer], b3.at[w, z], where).wait_send()
        return 0

    lax.fori_loop(0, nz - 1, sent, 0)


def per_device(values, dt_raw, dt_bias, decay_rate, features, bc_weight, out_grad):
    nz = lax.axis_size("ctx") // 4
    tokens, heads = dt_raw.shape[1:]
    feats = features.shape[2]
    two_n = bc_weight.shape[1]
    plan = scratch_plan(nz, tokens, heads, feats, two_n)
    outs = pl.pallas_call(
        make_kernel(list(plan)),
        out_shape=(
            jax.ShapeDtypeStruct(values.shape[1:], BF16),
            jax.ShapeDtypeStruct((tokens, heads), F32),
            jax.ShapeDtypeStruct((tokens, feats), BF16),
            jax.ShapeDtypeStruct((2, feats), F32),
        ),
        in_specs=[VMEM] * 7,
        out_specs=(VMEM,) * 4,
        scratch_shapes=list(plan.values()),
        compiler_params=pltpu.CompilerParams(
            collective_id=0, has_side_effects=True, vmem_limit_bytes=48 << 20
        ),
        name="layer_backward",
    )(values[0], dt_raw[0], dt_bias[None], decay_rate[None], features[0], bc_weight, out_grad[0])
    return (outs[0][None], outs[1][None], outs[2][None], outs[3])


def solution(mesh):
    return jax.shard_map(
        per_device,
        mesh=mesh,
        in_specs=(
            P("dp", "ctx", "head"),
            P("dp", "ctx", "head"),
            P("head"),
            P("head"),
            P("dp", "ctx", "head"),
            P("head", None),
            P("dp", "ctx", "head"),
        ),
        out_specs=(
            P("dp", "ctx", "head"),
            P("dp", "ctx", "head"),
            P("dp", "ctx", "head"),
            P(("ctx", "dp"), "head"),
        ),
        check_vma=False,
    )
```

time: 1020 us -> 83.1 us (0.08)
  waiting for transfers between devices: 564 us -> 0 us
  local copies, waits for them, and re-layouts: 166 us -> 8.38 us
  other arithmetic: 157 us -> 0 us
  blocking collectives: 91 us -> 0 us
  Pallas kernels: 0 us -> 73.8 us
  matrix products: 16.5 us -> 0 us
  between operations: 14.6 us -> 0.67 us
    unnamed x7 -> x0, waiting for transfers between devices: 373 us -> none
    all_gather x2 -> x0, waiting for transfers between devices: 162 us -> none  [carried_in(): everything = jax.tree.map(lambda part: lax.all_gather(part, axis), shard)]
    mul x129 -> x0, local copies, waits for them, and re-layouts: 153 us -> none  [the longest x128 153 us: combine(): later[0][:, None, None] * earlier[1] + later[1]]
    select_n x128 -> x0, other arithmetic: 150 us -> none  [lap(): return jax.tree.map(lambda a, b: jnp.where(reached, a, b), new, before)]
    all_gather x3 -> x0, blocking collectives: 91 us -> none  [the longest x1 73.1 us: carried_in(): everything = jax.tree.map(lambda part: lax.all_gather(part, axis), shard)]
    pallas_call x0 -> x1, Pallas kernels: none -> 73.8 us  [per_device(): pl.pallas_call(make_kernel(list(plan)), out_shape=(jax.ShapeDtypeStruct(v...]
    reduce_scatter x1 -> x0, waiting for transfers between devices: 28.9 us -> none  [per_device(): lax.psum_scatter(part_sums, 'head', scatter_dimension=1, tiled=True)]
    dot_general x14 -> x0, matrix products: 16.5 us -> none  [the longest x2 4.01 us: block_forward(): inner_part = jnp.einsum('hts,shp->thp', mixing, scaled)]
  transfers between devices with their start and end apart: 5 -> 0, of which waited for: 5 -> 0; matrix products, arithmetic and copies ran while one was open for 17% -> 0% of each run, Pallas kernels for 0% -> 0%
where the time goes in v2:
time: 83.1 us; the launch traced here: 82.8 us
  Pallas kernels  73.8 us (89%)
  local copies, waits for them, and re-layouts  8.38 us (10%)
    pallas_call x1, Pallas kernels, per_device(): pl.pallas_call(make_kernel(list(plan)), out_shape=(jax.ShapeDtypeStruct(v...  73.8 us
    unnamed x19, local copies, waits for them, and re-layouts  8.38 us

profile of v2, /device:TPU:1, one launch (start us, length us, event | category | flops | bytes accessed | tf_op | source)
XLA Modules:
  0.0 82.8 jit_solution(18043819919233070239)
XLA Ops:
  0.6 0.0 copy-start.6
  0.6 0.7 copy-done.6
  1.3 0.1 copy.11
  1.4 0.0 copy-start.4
  1.4 0.0 copy-start.5
  1.4 0.6 copy-done.4
  2.1 0.0 copy-done.5
  2.1 0.0 copy-start
  2.1 1.2 %copy-done = bf16[2048,256]{1,0:T(8,128)(2,1)S(1)} copy-done((bf16[2048,256]{1,0:T(8,128)(2,1)S(1)}, bf16[2048,256]{1,0:T(8,128)(2,1)}, u32[]{:S(2)}) %copy-start) | copy-done | bytes 1048600
  3.3 0.0 copy-start.1
  3.3 1.0 %copy-done.1 = bf16[1,128,2048]{2,1,0:T(8,128)(2,1)S(1)} copy-done((bf16[1,128,2048]{2,1,0:T(8,128)(2,1)S(1)}, bf16[1,128,2048]{2,1,0:T(8,128)(2,1)}, u32[]{:S(2)}) %copy-start.1) | copy-done | bytes 524312
  4.4 0.0 copy-start.2
  4.4 0.9 %copy-done.2 = bf16[1,128,1024]{2,1,0:T(8,128)(2,1)S(1)} copy-done((bf16[1,128,1024]{2,1,0:T(8,128)(2,1)S(1)}, bf16[1,128,1024]{2,1,0:T(8,128)(2,1)}, u32[]{:S(2)}) %copy-start.2) | copy-done | bytes 262168
  5.3 0.0 copy-start.3
  5.3 0.9 %copy-done.3 = bf16[1,128,1024]{2,1,0:T(8,128)(2,1)S(1)} copy-done((bf16[1,128,1024]{2,1,0:T(8,128)(2,1)S(1)}, bf16[1,128,1024]{2,1,0:T(8,128)(2,1)}, u32[]{:S(2)}) %copy-start.3) | copy-done | bytes 262168
  6.3 73.8 %layer_backward.1 = (bf16[128,1024]{1,0:T(8,128)(2,1)S(1)}, f32[128,16]{1,0:T(8,128)S(1)}, bf16[128,2048]{1,0:T(8,128)(2,1)S(1)}, f32[2,2048]{1,0:T(2,128)S(1)}) custom-call(bf16[128,1024]{1,0:T(8,128)(2,1)S(1)} %bitcast.13, f32[128,16]{1,0:T(8,128)S(1)} %bitcast.11, f32[1,16]{1,0:T(1,128)S(1)} %bitcast.16, f32[1,16]{1,0:T(1,128)S(1)} %bitcast.17, ...), custom_call_target="tpu_custom_call" | custom-call | tf_op jit(solution)/shard_map/layer_backward/pallas_call | solution.py:474
  80.0 0.7 copy.12
  80.7 0.7 copy.16
  81.4 0.8 copy.17
  82.2 0.6 copy.18
Async XLA Ops:
  0.6 0.7 copy-start.6
  1.4 0.7 copy-start.4
  1.4 0.7 copy-start.5
  2.1 1.2 %copy-start = (bf16[2048,256]{1,0:T(8,128)(2,1)S(1)}, bf16[2048,256]{1,0:T(8,128)(2,1)}, u32[]{:S(2)}) copy-start(bf16[2048,256]{1,0:T(8,128)(2,1)} %weight.1) | copy-start | bytes 3145732
  3.3 1.0 %copy-start.1 = (bf16[1,128,2048]{2,1,0:T(8,128)(2,1)S(1)}, bf16[1,128,2048]{2,1,0:T(8,128)(2,1)}, u32[]{:S(2)}) copy-start(bf16[1,128,2048]{2,1,0:T(8,128)(2,1)} %param.11) | copy-start | bytes 1572868
  4.4 0.9 %copy-start.2 = (bf16[1,128,1024]{2,1,0:T(8,128)(2,1)S(1)}, bf16[1,128,1024]{2,1,0:T(8,128)(2,1)}, u32[]{:S(2)}) copy-start(bf16[1,128,1024]{2,1,0:T(8,128)(2,1)} %param.7) | copy-start | bytes 786436
  5.3 0.9 %copy-start.3 = (bf16[1,128,1024]{2,1,0:T(8,128)(2,1)S(1)}, bf16[1,128,1024]{2,1,0:T(8,128)(2,1)}, u32[]{:S(2)}) copy-start(bf16[1,128,1024]{2,1,0:T(8,128)(2,1)} %param.13) | copy-start | bytes 786436

commit v3 on v2

v3 whole, which is shorter than its diff:
```python
import jax
import jax.numpy as jnp
from jax import lax
from jax.experimental import pallas as pl
from jax.experimental.pallas import tpu as pltpu
from jax.sharding import PartitionSpec as P

F32 = jnp.float32
BF16 = jnp.bfloat16
EXACT = lax.Precision.HIGHEST
MESH_ID = pl.DeviceIdType.MESH
VMEM = pl.BlockSpec(memory_space=pltpu.VMEM)
HBM = pl.BlockSpec(memory_space=pltpu.HBM)
CHUNKS = 4
DMA = pltpu.SemaphoreType.DMA


def remote(src, dst, send_sem, recv_sem, where):
    return pltpu.make_async_remote_copy(
        src_ref=src, dst_ref=dst, send_sem=send_sem, recv_sem=recv_sem,
        device_id=where, device_id_type=MESH_ID,
    )


def greet(barrier, where):
    pl.semaphore_signal(barrier, inc=1, device_id=where, device_id_type=MESH_ID)


def far_first(k, nz):
    return nz // 2 + (1 - 2 * (k % 2)) * ((k + 1) // 2)


def dot(a, b, ca, cb, precision=None):
    return lax.dot_general(
        a, b, (((ca,), (cb,)), ((), ())), precision=precision, preferred_element_type=F32
    )


def iota(shape, dim):
    return lax.broadcasted_iota(jnp.int32, shape, dim)


def scratch_plan(nz, tokens, heads, feats, two_n):
    rows = 128 // nz
    part = feats // CHUNKS
    block = two_n // 8
    wide = heads * 64
    return dict(
        values=pltpu.VMEM((tokens, wide), BF16),
        raw_t=pltpu.VMEM((heads, tokens), F32),
        bias=pltpu.VMEM((1, heads), F32),
        rate=pltpu.VMEM((1, heads), F32),
        features=pltpu.VMEM((tokens, feats), BF16),
        weight=pltpu.VMEM((feats, two_n), BF16),
        out_grad=pltpu.VMEM((tokens, wide), BF16),
        fetched=DMA((7,)),
        ha=pltpu.VMEM((2, tokens, two_n // 2), BF16),
        hb=pltpu.VMEM((2, tokens, two_n // 2), BF16),
        ga=pltpu.VMEM((2, 3, tokens, two_n // 2), BF16),
        gb=pltpu.VMEM((2, 3, tokens, two_n // 2), BF16),
        ha_s=DMA((2, 3)), ha_r=DMA((2, 3)), hb_s=DMA((2, 3)), hb_r=DMA((2, 3)),
        lg=pltpu.VMEM((4, 1, 256), F32),
        ld=pltpu.VMEM((4, 1, 256), F32),
        zl=pltpu.VMEM((2, 1, 128), F32),
        zd=pltpu.VMEM((nz, 2, 1, 128), F32),
        lg_s=DMA((3,)), lg_r=DMA((4,)), zl_s=DMA((nz,)), zl_r=DMA((nz,)),
        vin=pltpu.VMEM((tokens, wide), BF16),
        gin=pltpu.VMEM((tokens, wide), BF16),
        sg=pltpu.VMEM((2, 128, wide), BF16),
        r1=pltpu.VMEM((4, 4, 128, 128), BF16),
        zs=pltpu.VMEM((4, nz, rows, 128), BF16),
        r2=pltpu.VMEM((4, nz, rows, 128), BF16),
        bk=pltpu.VMEM((4, nz, rows, 128), BF16),
        r4=pltpu.VMEM((4, nz, rows, 128), BF16),
        p5=pltpu.VMEM((4, 4, 128, 128), BF16),
        r5=pltpu.VMEM((4, 4, 128, 128), BF16),
        s1=DMA((4, 3)), g1=DMA((4, 4)), s2=DMA((4, nz)), g2=DMA((4, nz)),
        s4=DMA((4, nz)), g4=DMA((4, nz)), s5=DMA((4, 3)), g5=DMA((4, 4)),
        dx=pltpu.VMEM((tokens, wide), F32),
        drow=pltpu.VMEM((tokens, tokens), F32),
        pt=pltpu.VMEM((two_n, tokens), BF16),
        w0=pltpu.VMEM((CHUNKS, two_n // 2, part), BF16),
        w1=pltpu.VMEM((CHUNKS, two_n // 2, part), F32),
        e1=pltpu.VMEM((CHUNKS, two_n // 2, part), BF16),
        hs=pltpu.VMEM((CHUNKS, 3, block, part), BF16),
        e2=pltpu.VMEM((CHUNKS, 3, block, part), BF16),
        ws=pltpu.VMEM((CHUNKS, nz, 2, part), BF16),
        e3=pltpu.VMEM((CHUNKS, nz, 2, part), BF16),
        a1=DMA((CHUNKS,)), b1=DMA((CHUNKS,)), a2=DMA((CHUNKS, 3)), b2=DMA((CHUNKS, 3)),
        a3=DMA((CHUNKS, nz)), b3=DMA((CHUNKS, nz)),
    )


def make_kernel(names):
    def kernel(*refs):
        step(refs[:7], refs[7:11], **dict(zip(names, refs[11:])))
    return kernel


def step(held, results, *,
         values, raw_t, bias, rate, features, weight, out_grad, fetched,
         ha, hb, ga, gb, ha_s, ha_r, hb_s, hb_r,
         lg, ld, zl, zd, lg_s, lg_r, zl_s, zl_r,
         vin, gin, sg, r1, zs, r2, bk, r4, p5, r5, s1, g1, s2, g2, s4, g4, s5, g5,
         dx, drow, pt, w0, w1, e1, hs, e2, ws, e3, a1, b1, a2, b2, a3, b3):
    grad_values, grad_dt, grad_features, grad_weight = results
    here = (values, raw_t, bias, rate, features, weight, out_grad)
    fetches = [
        pltpu.make_async_copy(held[i], here[i], fetched.at[i]) for i in range(7)
    ]
    for i in (5, 4, 1, 2, 3, 0, 6):
        fetches[i].start()
    ctx, head, dp = lax.axis_index("ctx"), lax.axis_index("head"), lax.axis_index("dp")
    nz = zd.shape[0]
    z, p = ctx // 4, ctx % 4
    low, core = (ctx // 2) % 2, ctx % 2
    y = dp * 2 + low
    rows = 128 // nz
    heads, tokens = raw_t.shape
    pairs = heads // 2
    state = 128
    part = features.shape[1] // CHUNKS
    block = weight.shape[1] // 8

    def at_head(d):
        return {"head": (head + d) % 4}

    def in_plane(d):
        return {"ctx": z * 4 + (p + d) % 4}

    def along_z(peer):
        return {"ctx": peer * 4 + p}

    def along_y(d):
        to = (y + d) % 4
        return {"ctx": z * 4 + (to % 2) * 2 + core, "dp": to // 2}

    other = {"ctx": ctx + 1 - 2 * core}

    barrier = pltpu.get_barrier_semaphore()

    def hello(k, _):
        greet(barrier, along_z((z + far_first(k, nz)) % nz))
        return 0

    lax.fori_loop(0, nz - 1, hello, 0)
    for d in (2, 1, 3):
        greet(barrier, along_y(d))
        greet(barrier, at_head(d))
        greet(barrier, in_plane(d))

    fetches[5].wait()
    fetches[4].wait()
    partial = dot(features[...], weight[...], 1, 0).astype(BF16)
    ha[0] = partial[:, :state]
    ha[1] = partial[:, state:]

    for i in (1, 2, 3):
        fetches[i].wait()

    def flip(few):
        return jnp.concatenate([few, jnp.zeros((128 - heads, tokens), F32)], axis=0).T[:, :heads]

    pre = flip(raw_t[...]) + bias[...]
    dt = jax.nn.softplus(pre)
    lower = (iota((tokens, tokens), 0) >= iota((tokens, tokens), 1)).astype(F32)
    run = dot(lower, -dt * rate[...], 1, 0, EXACT)
    last = run[tokens - 1:tokens, :]
    into = jnp.exp(run)
    tail = jnp.exp(last - run)
    ends = jnp.exp(last)
    run_t = jnp.concatenate([run, jnp.zeros((tokens, 128 - heads), F32)], axis=1).T
    first_half = iota((tokens, 128), 1) < 64

    def spread(cols, j):
        return jnp.where(first_half, cols[:, 2 * j:2 * j + 1], cols[:, 2 * j + 1:2 * j + 2])

    row_half = iota((1, 128), 1) < 64
    for j in range(pairs):
        lg[j // 2, :, 128 * (j % 2):128 * (j % 2) + 128] = jnp.where(
            row_half, last[:, 2 * j:2 * j + 1], last[:, 2 * j + 1:2 * j + 2]
        )
    dt_tail = dt * tail
    fetches[0].wait()
    fetches[6].wait()
    for j in range(pairs):
        lanes = slice(128 * j, 128 * j + 128)
        vin[:, lanes] = (values[:, lanes].astype(F32) * spread(dt_tail, j)).astype(BF16)
        gin[:, lanes] = (out_grad[:, lanes].astype(F32) * spread(into, j)).astype(BF16)

    pl.semaphore_wait(barrier, nz - 1 + 9)

    def head_copy(src, dst, ss, rs, i, d):
        return remote(src.at[i], dst.at[i, d - 1], ss.at[i, d - 1], rs.at[i, d - 1], at_head(d))

    def head_total(src, dst, ss, rs, i):
        total = src[i].astype(F32)
        for d in (1, 3, 2):
            head_copy(src, dst, ss, rs, i, d).wait_recv()
            total = total + dst[i, d - 1].astype(F32)
        return total

    for i in range(2):
        for d in (2, 1, 3):
            head_copy(ha, ga, ha_s, ha_r, i, d).start()
    for d in (2, 3, 1):
        q = (p + d) % 4
        remote(lg.at[q], ld.at[p], lg_s.at[d - 1], lg_r.at[p], in_plane(d)).start()
    ld[p] = lg[p]
    for d in (1, 2, 3):
        q = (p + d) % 4
        remote(lg.at[q], ld.at[q], lg_s.at[d - 1], lg_r.at[q], in_plane(d)).wait_recv()
    whole = ld[0] + ld[1] + ld[2] + ld[3]
    zl[0] = whole[:, :128]
    zl[1] = whole[:, 128:]

    def send_decay(k, _):
        peer = (z + far_first(k, nz)) % nz
        remote(zl, zd.at[z], zl_s.at[peer], zl_r.at[z], along_z(peer)).start()
        return 0

    lax.fori_loop(0, nz - 1, send_decay, 0)
    zd[z] = zl[...]

    def plane_copy(w, d):
        q = (p + d) % 4
        lanes = pl.ds(pl.multiple_of(q * 256 + (w % 2) * 128, 128), 128)
        return remote(sg.at[w // 2, :, lanes], r1.at[w, p], s1.at[w, d - 1], g1.at[w, p], in_plane(d))

    halves = []
    for i, fed in ((0, vin), (1, gin)):
        total = head_total(ha, ga, ha_s, ha_r, i)
        halves.append(total.astype(BF16))
        turned = halves[i].astype(F32).T.astype(BF16)
        sg[i] = dot(turned, fed[...], 1, 0).astype(BF16)
        for w in (2 * i, 2 * i + 1):
            for d in (2, 3, 1):
                plane_copy(w, d).start()
            r1[w, p] = sg[i, :, pl.ds(pl.multiple_of(p * 256 + (w % 2) * 128, 128), 128)]
    b_proj, c_proj = halves

    def plane_wait(buf, rs, ss, w):
        for d in (1, 3, 2):
            q = (p + d) % 4
            remote(buf.at[w, q], buf.at[w, q], ss.at[w, d - 1], rs.at[w, q], in_plane(d)).wait_recv()

    decays = [jnp.exp(ld[q]) for q in range(4)]

    def order_of(w):
        return (0, 1, 2, 3) if w < 2 else (3, 2, 1, 0)

    def decay_of(w, q):
        return decays[q][:, 128 * (w % 2):128 * (w % 2) + 128]

    def combine(w):
        order = order_of(w)
        acc = r1[w, order[0]].astype(F32)
        for q in order[1:]:
            acc = acc * decay_of(w, q) + r1[w, q].astype(F32)
        for j in range(nz):
            zs[w, j] = acc[j * rows:j * rows + rows].astype(BF16)

    def z_send(src, dst, ss, rs, w):
        def go(k, _):
            peer = (z + far_first(k, nz)) % nz
            remote(src.at[w, peer], dst.at[w, z], ss.at[w, peer], rs.at[w, z], along_z(peer)).start()
            return 0

        lax.fori_loop(0, nz - 1, go, 0)
        dst[w, z] = src[w, z]

    def z_wait(src, dst, ss, rs, w):
        def go(k, _):
            peer = (z + 1 + k) % nz
            remote(src.at[w, peer], dst.at[w, peer], ss.at[w, peer], rs.at[w, peer],
                   along_z(peer)).wait_recv()
            return 0

        lax.fori_loop(0, nz - 1, go, 0)

    for w in range(4):
        plane_wait(r1, g1, s1, w)
        combine(w)
        z_send(zs, r2, s2, g2, w)

    scores_t = dot(b_proj, c_proj, 1, 1)
    causal_t = iota((tokens, tokens), 0) <= iota((tokens, tokens), 1)
    strict_t = iota((tokens, tokens), 0) < iota((tokens, tokens), 1)
    strict_scores = jnp.where(strict_t, scores_t, 0.0)
    lane = iota((tokens, heads), 1)
    drow[...] = jnp.zeros_like(drow)

    def local_pairs(lo, hi, dscore, dcol):
        for j in range(lo, hi):
            lanes = slice(128 * j, 128 * j + 128)
            grads = out_grad[:, lanes]
            zero = jnp.zeros_like(grads)
            split = jnp.concatenate(
                [jnp.where(first_half, grads, zero), jnp.where(first_half, zero, grads)], axis=0
            )
            products = dot(values[:, lanes], split, 1, 1)
            mixes = []
            for i in range(2):
                h = 2 * j + i
                gap = run_t[h:h + 1, :] - run[:, h:h + 1]
                fall = jnp.exp(jnp.where(causal_t, gap, -1e30))
                mixes.append((fall * scores_t).astype(BF16))
                part = fall * (products[:, 128 * i:128 * i + 128] * dt[:, h:h + 1])
                dscore = dscore + part
                part = part * strict_scores
                drow[h:h + 1, :] = jnp.sum(part, axis=0, keepdims=True)
                dcol = jnp.where(lane == h, jnp.sum(part, axis=1, keepdims=True), dcol)
            dx[:, lanes] = dot(jnp.concatenate(mixes, axis=1), split, 1, 0)
        return dscore, dcol

    dscore = jnp.zeros((tokens, tokens), F32)
    dcol = jnp.zeros((tokens, heads), F32)
    dscore, dcol = local_pairs(0, pairs // 2, dscore, dcol)

    def owner_scan(w):
        carry = jnp.zeros((rows, 128), F32)
        for k in range(nz):
            m = k if w < 2 else nz - 1 - k
            bk[w, m] = carry.astype(BF16)
            carry = carry * jnp.exp(zd[m, w % 2]) + r2[w, m].astype(F32)

    def decay_wait(k, _):
        peer = (z + 1 + k) % nz
        remote(zl, zd.at[peer], zl_s.at[peer], zl_r.at[peer], along_z(peer)).wait_recv()
        return 0

    lax.fori_loop(0, nz - 1, decay_wait, 0)
    for w in range(4):
        z_wait(zs, r2, s2, g2, w)
        owner_scan(w)
        z_send(bk, r4, s4, g4, w)

    dscore, dcol = local_pairs(pairs // 2, pairs, dscore, dcol)
    dscore_t = dscore.astype(BF16)
    dscore_n = dscore.T.astype(BF16)
    grad_b = dot(dscore_t, c_proj, 1, 0)
    grad_c = dot(dscore_n, b_proj, 1, 0)
    dr = drow[...].T[:, :heads] - dcol

    def expand(w):
        for j in range(nz):
            span = slice(j * rows, j * rows + rows)
            carry = r4[w, j].astype(F32)
            for n, q in enumerate(order_of(w)):
                p5[w, q, span, :] = carry.astype(BF16)
                if n < 3:
                    carry = carry * decay_of(w, q) + r1[w, q, span, :].astype(F32)

    def back_copy(w, d):
        q = (p + d) % 4
        return remote(p5.at[w, q], r5.at[w, p], s5.at[w, d - 1], g5.at[w, p], in_plane(d))

    for w in range(4):
        z_wait(bk, r4, s4, g4, w)
        expand(w)
        for d in (2, 3, 1):
            back_copy(w, d).start()
        r5[w, p] = p5[w, p]

    group = (iota((256, 128), 0) // 64) == iota((256, 128), 1)
    groups = group.astype(F32)

    def head_sums(wide_rows):
        return dot(wide_rows, groups, 1, 0, EXACT)[:, :4]

    def entering(i, q):
        return jnp.concatenate([r5[2 * i, q], r5[2 * i + 1, q]], axis=1)

    plane_wait(r5, g5, s5, 0)
    plane_wait(r5, g5, s5, 1)
    for q in range(4):
        grad_c = grad_c + dot(gin[:, 256 * q:256 * q + 256], entering(0, q), 1, 1)
    hb[1] = grad_c.astype(BF16)
    for d in (2, 1, 3):
        head_copy(hb, gb, hb_s, hb_r, 1, d).start()
    gains = []
    for q in range(4):
        lanes = slice(256 * q, 256 * q + 256)
        gains.append(head_sums(dot(c_proj, entering(0, q), 1, 0) * gin[:, lanes].astype(F32)))
    dr = dr + jnp.concatenate(gains, axis=1)

    plane_wait(r5, g5, s5, 2)
    plane_wait(r5, g5, s5, 3)
    for q in range(4):
        grad_b = grad_b + dot(vin[:, 256 * q:256 * q + 256], entering(1, q), 1, 1)
    hb[0] = grad_b.astype(BF16)
    for d in (2, 1, 3):
        head_copy(hb, gb, hb_s, hb_r, 0, d).start()

    falls, value_dots, kept = [], [], []
    for q in range(4):
        lanes = slice(256 * q, 256 * q + 256)
        exits = entering(1, q)
        reach = dot(b_proj, exits, 1, 0)
        falls.append(head_sums(reach * vin[:, lanes].astype(F32)))
        wide_tail = jnp.concatenate([spread(tail, 2 * q), spread(tail, 2 * q + 1)], axis=1)
        full = dx[:, lanes] + reach * wide_tail
        kept.append(head_sums(jnp.sum(
            exits.astype(F32) * entering(0, q).astype(F32), axis=0, keepdims=True
        )))
        value_dots.append(head_sums(full * values[:, lanes].astype(F32)))
        wide_dt = jnp.concatenate([spread(dt, 2 * q), spread(dt, 2 * q + 1)], axis=1)
        grad_values[:, lanes] = (full * wide_dt).astype(BF16)
    fall = jnp.concatenate(falls, axis=1)
    dr = dr - fall
    at_end = jnp.sum(fall, axis=0, keepdims=True) + ends * jnp.concatenate(kept, axis=1)
    upper = (iota((tokens, tokens), 0) <= iota((tokens, tokens), 1)).astype(F32)
    dlog = dot(upper, dr, 1, 0, EXACT) + at_end
    grads = (jnp.concatenate(value_dots, axis=1) - rate[...] * dlog) * jax.nn.sigmoid(pre)
    grad_dt[...] = jnp.concatenate([grads, jnp.zeros((tokens, 128 - heads), F32)], axis=1).T[:heads]

    grad_cs = head_total(hb, gb, hb_s, hb_r, 1).astype(BF16)
    grad_bs = head_total(hb, gb, hb_s, hb_r, 0).astype(BF16)
    rounded = jnp.concatenate([grad_bs, grad_cs], axis=1)

    new_row = iota((2 * state, 2 * state), 0)
    inner = 2 * state // (8 * nz)
    old_row = (
        ((new_row // inner) % nz) * (8 * inner)
        + ((new_row // (inner * nz)) % 2) * (4 * inner)
        + (new_row // (4 * inner * nz)) * (2 * inner)
        + ((new_row // (2 * inner * nz)) % 2) * inner
        + new_row % inner
    )
    pick = (iota((2 * state, 2 * state), 1) == old_row).astype(BF16)
    pt[...] = dot(pick, rounded, 1, 1).astype(BF16)
    theirs = pt[pl.ds(pl.multiple_of((1 - core) * state, state), state), :]
    ours = pt[pl.ds(pl.multiple_of(core * state, state), state), :]

    def pair_copy(c):
        return remote(w0.at[c], e1.at[c], a1.at[c], b1.at[c], other)

    def y_copy(c, d):
        return remote(hs.at[c, d - 1], e2.at[c, d - 1], a2.at[c, d - 1], b2.at[c, d - 1], along_y(d))

    for c in range(CHUNKS):
        w0[c] = dot(theirs, features[:, part * c:part * c + part], 1, 0).astype(BF16)
        pair_copy(c).start()
    for c in range(CHUNKS):
        w1[c] = dot(ours, features[:, part * c:part * c + part], 1, 0)
    for c in range(CHUNKS):
        pair_copy(c).wait_recv()
        for d in (2, 1, 3):
            span = pl.ds(pl.multiple_of(((y + d) % 4) * block, block), block)
            hs[c, d - 1] = (w1[c, span, :] + e1[c, span, :].astype(F32)).astype(BF16)
            y_copy(c, d).start()

    grad_features[...] = dot(rounded, weight[...], 1, 1).astype(BF16)

    for c in range(CHUNKS):
        span = pl.ds(pl.multiple_of(y * block, block), block)
        total = w1[c, span, :] + e1[c, span, :].astype(F32)
        for d in (1, 3, 2):
            y_copy(c, d).wait_recv()
            total = total + e2[c, d - 1].astype(F32)
        for k in range(nz):
            ws[c, k] = total[2 * k:2 * k + 2].astype(BF16)
        z_send(ws, e3, a3, b3, c)
    for c in range(CHUNKS):
        z_wait(ws, e3, a3, b3, c)
        total = e3[c, 0].astype(F32)
        for k in range(1, nz):
            total = total + e3[c, k].astype(F32)
        grad_weight[:, part * c:part * c + part] = total

    for d in (1, 2, 3):
        q = (p + d) % 4
        for i in range(2):
            head_copy(ha, ga, ha_s, ha_r, i, d).wait_send()
            head_copy(hb, gb, hb_s, hb_r, i, d).wait_send()
        remote(lg.at[q], ld.at[p], lg_s.at[d - 1], lg_r.at[p], in_plane(d)).wait_send()
        for w in range(4):
            plane_copy(w, d).wait_send()
            back_copy(w, d).wait_send()
        for c in range(CHUNKS):
            y_copy(c, d).wait_send()
    for c in range(CHUNKS):
        pair_copy(c).wait_send()

    def sent(k, _):
        peer = (z + 1 + k) % nz
        where = along_z(peer)
        remote(zl, zd.at[z], zl_s.at[peer], zl_r.at[z], where).wait_send()
        for w in range(4):
            remote(zs.at[w, peer], r2.at[w, z], s2.at[w, peer], g2.at[w, z], where).wait_send()
            remote(bk.at[w, peer], r4.at[w, z], s4.at[w, peer], g4.at[w, z], where).wait_send()
        for c in range(CHUNKS):
            remote(ws.at[c, peer], e3.at[c, z], a3.at[c, peer], b3.at[c, z], where).wait_send()
        return 0

    lax.fori_loop(0, nz - 1, sent, 0)


def deliver_kernel(*refs):
    sems = refs[8]
    copies = [pltpu.make_async_copy(refs[i], refs[4 + i], sems.at[i]) for i in range(4)]
    for copy in copies:
        copy.start()
    for copy in copies:
        copy.wait()


def deliver(outs):
    return pl.pallas_call(
        deliver_kernel,
        out_shape=tuple(jax.ShapeDtypeStruct(o.shape, o.dtype) for o in outs),
        in_specs=[VMEM] * 4,
        out_specs=(HBM,) * 4,
        scratch_shapes=[DMA((4,))],
        compiler_params=pltpu.CompilerParams(vmem_limit_bytes=8 << 20),
        name="deliver",
    )(*outs)


def per_device(values, dt_raw, dt_bias, decay_rate, features, bc_weight, out_grad):
    nz = lax.axis_size("ctx") // 4
    tokens, heads = dt_raw.shape[1:]
    feats = features.shape[2]
    two_n = bc_weight.shape[1]
    plan = scratch_plan(nz, tokens, heads, feats, two_n)
    outs = pl.pallas_call(
        make_kernel(list(plan)),
        out_shape=(
            jax.ShapeDtypeStruct(values.shape[1:], BF16),
            jax.ShapeDtypeStruct((heads, tokens), F32),
            jax.ShapeDtypeStruct((tokens, feats), BF16),
            jax.ShapeDtypeStruct((2, feats), F32),
        ),
        in_specs=[HBM] * 7,
        out_specs=(VMEM,) * 4,
        scratch_shapes=list(plan.values()),
        compiler_params=pltpu.CompilerParams(
            collective_id=0, has_side_effects=True, vmem_limit_bytes=48 << 20
        ),
        name="layer_backward",
    )(*[pltpu.with_memory_space_constraint(x, pltpu.HBM) for x in (
        values[0], dt_raw[0].T, dt_bias[None], decay_rate[None], features[0], bc_weight, out_grad[0]
    )])
    outs = deliver(outs)
    return (outs[0][None], outs[1].T[None], outs[2][None], outs[3])


def solution(mesh):
    return jax.shard_map(
        per_device,
        mesh=mesh,
        in_specs=(
            P("dp", "ctx", "head"),
            P("dp", "ctx", "head"),
            P("head"),
            P("head"),
            P("dp", "ctx", "head"),
            P("head", None),
            P("dp", "ctx", "head"),
        ),
        out_specs=(
            P("dp", "ctx", "head"),
            P("dp", "ctx", "head"),
            P("dp", "ctx", "head"),
            P(("ctx", "dp"), "head"),
        ),
        check_vma=False,
    )
```

time: 83.1 us -> 73.5 us (0.88)
  local copies, waits for them, and re-layouts: 8.38 us -> 0 us
  Pallas kernels: 73.8 us -> 72.7 us
    unnamed x19 -> x0, local copies, waits for them, and re-layouts: 8.38 us -> none
    pallas_call x1, Pallas kernels: 73.8 us -> 71.7 us  [per_device(): pl.pallas_call(make_kernel(list(plan)), out_shape=(jax.ShapeDtypeStruct(v...]
    pallas_call x0 -> x1, Pallas kernels: none -> 0.92 us  [deliver(): pl.pallas_call(deliver_kernel, out_shape=tuple((jax.ShapeDtypeStruct(o.sh...]
where the time goes in v3:
time: 73.5 us; the launch traced here: 73.3 us
  Pallas kernels  72.7 us (99%)
    pallas_call x1, Pallas kernels, per_device(): pl.pallas_call(make_kernel(list(plan)), out_shape=(jax.ShapeDtypeStruct(v...  71.7 us

profile of v3, /device:TPU:1, one launch (start us, length us, event | category | flops | bytes accessed | tf_op | source)
XLA Modules:
  0.0 73.3 jit_solution(17657793035525052469)
XLA Ops:
  0.6 71.7 %layer_backward.1 = (bf16[128,1024]{1,0:T(8,128)(2,1)S(1)}, f32[16,128]{1,0:T(8,128)S(1)}, bf16[128,2048]{1,0:T(8,128)(2,1)S(1)}, f32[2,2048]{1,0:T(2,128)S(1)}) custom-call(bf16[128,1024]{1,0:T(8,128)(2,1)} %bitcast.14, f32[16,128]{1,0:T(8,128)} %bitcast.16, f32[1,16]{1,0:T(1,128)} %bitcast.17, f32[1,16]{1,0:T(1,128)} %bitcast.18, ...), custom_call_target="tpu_custom_call" | custom-call | tf_op jit(solution)/shard_map/layer_backward/pallas_call | solution.py:526
  72.4 0.9 %deliver.1 = (bf16[128,1024]{1,0:T(8,128)(2,1)}, f32[16,128]{1,0:T(8,128)}, bf16[128,2048]{1,0:T(8,128)(2,1)}, f32[2,2048]{1,0:T(2,128)}) custom-call(bf16[128,1024]{1,0:T(8,128)(2,1)S(1)} %get-tuple-element.12.refs_0_, f32[16,128]{1,0:T(8,128)S(1)} %get-tuple-element.13.refs_1_, bf16[128,2048]{1,0:T(8,128)(2,1)S(1)} %get-tuple-element.14.refs_2_, ...), custom_call_target="tpu_custom_call" | custom-call | tf_op jit(solution)/shard_map/deliver/pallas_call | solution.py:509

commit v4 on v3

--- a/solution.py
+++ b/solution.py
@@ -50,10 +50,11 @@
         raw_t=pltpu.VMEM((heads, tokens), F32),
         bias=pltpu.VMEM((1, heads), F32),
         rate=pltpu.VMEM((1, heads), F32),
-        features=pltpu.VMEM((tokens, feats), BF16),
+        features=pltpu.VMEM((2, tokens, feats), BF16),
         weight=pltpu.VMEM((feats, two_n), BF16),
         out_grad=pltpu.VMEM((tokens, wide), BF16),
         fetched=DMA((7,)),
+        relay=pltpu.SemaphoreType.REGULAR((max(nz.bit_length() - 2, 1),)),
         ha=pltpu.VMEM((2, tokens, two_n // 2), BF16),
         hb=pltpu.VMEM((2, tokens, two_n // 2), BF16),
         ga=pltpu.VMEM((2, 3, tokens, two_n // 2), BF16),
@@ -79,14 +80,13 @@
         dx=pltpu.VMEM((tokens, wide), F32),
         drow=pltpu.VMEM((tokens, tokens), F32),
         pt=pltpu.VMEM((two_n, tokens), BF16),
-        w0=pltpu.VMEM((CHUNKS, two_n // 2, part), BF16),
         w1=pltpu.VMEM((CHUNKS, two_n // 2, part), F32),
-        e1=pltpu.VMEM((CHUNKS, two_n // 2, part), BF16),
+        e1=pltpu.VMEM((two_n // 2, tokens), BF16),
         hs=pltpu.VMEM((CHUNKS, 3, block, part), BF16),
         e2=pltpu.VMEM((CHUNKS, 3, block, part), BF16),
         ws=pltpu.VMEM((CHUNKS, nz, 2, part), BF16),
         e3=pltpu.VMEM((CHUNKS, nz, 2, part), BF16),
-        a1=DMA((CHUNKS,)), b1=DMA((CHUNKS,)), a2=DMA((CHUNKS, 3)), b2=DMA((CHUNKS, 3)),
+        f_s=DMA((1,)), f_r=DMA((1,)), a1=DMA((1,)), b1=DMA((1,)), a2=DMA((CHUNKS, 3)), b2=DMA((CHUNKS, 3)),
         a3=DMA((CHUNKS, nz)), b3=DMA((CHUNKS, nz)),
     )
 
@@ -98,13 +98,13 @@
 
 
 def step(held, results, *,
-         values, raw_t, bias, rate, features, weight, out_grad, fetched,
+         values, raw_t, bias, rate, features, weight, out_grad, fetched, relay,
          ha, hb, ga, gb, ha_s, ha_r, hb_s, hb_r,
          lg, ld, zl, zd, lg_s, lg_r, zl_s, zl_r,
          vin, gin, sg, r1, zs, r2, bk, r4, p5, r5, s1, g1, s2, g2, s4, g4, s5, g5,
-         dx, drow, pt, w0, w1, e1, hs, e2, ws, e3, a1, b1, a2, b2, a3, b3):
+         dx, drow, pt, w1, e1, hs, e2, ws, e3, f_s, f_r, a1, b1, a2, b2, a3, b3):
     grad_values, grad_dt, grad_features, grad_weight = results
-    here = (values, raw_t, bias, rate, features, weight, out_grad)
+    here = (values, raw_t, bias, rate, features.at[0], weight, out_grad)
     fetches = [
         pltpu.make_async_copy(held[i], here[i], fetched.at[i]) for i in range(7)
     ]
@@ -119,7 +119,7 @@
     heads, tokens = raw_t.shape
     pairs = heads // 2
     state = 128
-    part = features.shape[1] // CHUNKS
+    part = features.shape[2] // CHUNKS
     block = weight.shape[1] // 8
 
     def at_head(d):
@@ -138,22 +138,47 @@
     other = {"ctx": ctx + 1 - 2 * core}
 
     barrier = pltpu.get_barrier_semaphore()
-
-    def hello(k, _):
-        greet(barrier, along_z((z + far_first(k, nz)) % nz))
-        return 0
-
-    lax.fori_loop(0, nz - 1, hello, 0)
+    for d in (2, 1, 3):
+        greet(barrier, at_head(d))
+    for d in (1, nz - 1):
+        greet(barrier, along_z((z + d) % nz))
     for d in (2, 1, 3):
         greet(barrier, along_y(d))
-        greet(barrier, at_head(d))
         greet(barrier, in_plane(d))
 
     fetches[5].wait()
     fetches[4].wait()
-    partial = dot(features[...], weight[...], 1, 0).astype(BF16)
+    partial = dot(features[0], weight[...], 1, 0).astype(BF16)
     ha[0] = partial[:, :state]
     ha[1] = partial[:, state:]
+
+    pl.semaphore_wait(barrier, 11)
+
+    reaches = [1 << i for i in range(nz.bit_length() - 2)]
+
+    def relay_signal(i):
+        for d in (reaches[i], nz - reaches[i]):
+            pl.semaphore_signal(
+                relay.at[i], inc=1, device_id=along_z((z + d) % nz), device_id_type=MESH_ID
+            )
+
+    def relay_wait(i):
+        pl.semaphore_wait(relay.at[i], 2)
+
+    def head_copy(src, dst, ss, rs, i, d):
+        return remote(src.at[i], dst.at[i, d - 1], ss.at[i, d - 1], rs.at[i, d - 1], at_head(d))
+
+    def head_total(src, dst, ss, rs, i):
+        total = src[i].astype(F32)
+        for d in (1, 3, 2):
+            head_copy(src, dst, ss, rs, i, d).wait_recv()
+            total = total + dst[i, d - 1].astype(F32)
+        return total
+
+    for i in range(2):
+        for d in (2, 1, 3):
+            head_copy(ha, ga, ha_s, ha_r, i, d).start()
+    relay_signal(0)
 
     for i in (1, 2, 3):
         fetches[i].wait()
@@ -188,39 +213,12 @@
         vin[:, lanes] = (values[:, lanes].astype(F32) * spread(dt_tail, j)).astype(BF16)
         gin[:, lanes] = (out_grad[:, lanes].astype(F32) * spread(into, j)).astype(BF16)
 
-    pl.semaphore_wait(barrier, nz - 1 + 9)
-
-    def head_copy(src, dst, ss, rs, i, d):
-        return remote(src.at[i], dst.at[i, d - 1], ss.at[i, d - 1], rs.at[i, d - 1], at_head(d))
-
-    def head_total(src, dst, ss, rs, i):
-        total = src[i].astype(F32)
-        for d in (1, 3, 2):
-            head_copy(src, dst, ss, rs, i, d).wait_recv()
-            total = total + dst[i, d - 1].astype(F32)
-        return total
-
-    for i in range(2):
-        for d in (2, 1, 3):
-            head_copy(ha, ga, ha_s, ha_r, i, d).start()
     for d in (2, 3, 1):
         q = (p + d) % 4
         remote(lg.at[q], ld.at[p], lg_s.at[d - 1], lg_r.at[p], in_plane(d)).start()
-    ld[p] = lg[p]
-    for d in (1, 2, 3):
-        q = (p + d) % 4
-        remote(lg.at[q], ld.at[q], lg_s.at[d - 1], lg_r.at[q], in_plane(d)).wait_recv()
-    whole = ld[0] + ld[1] + ld[2] + ld[3]
-    zl[0] = whole[:, :128]
-    zl[1] = whole[:, 128:]
-
-    def send_decay(k, _):
-        peer = (z + far_first(k, nz)) % nz
-        remote(zl, zd.at[z], zl_s.at[peer], zl_r.at[z], along_z(peer)).start()
-        return 0
-
-    lax.fori_loop(0, nz - 1, send_decay, 0)
-    zd[z] = zl[...]
+    for i in range(len(reaches) - 1):
+        relay_wait(i)
+        relay_signal(i + 1)
 
     def plane_copy(w, d):
         q = (p + d) % 4
@@ -244,8 +242,6 @@
             q = (p + d) % 4
             remote(buf.at[w, q], buf.at[w, q], ss.at[w, d - 1], rs.at[w, q], in_plane(d)).wait_recv()
 
-    decays = [jnp.exp(ld[q]) for q in range(4)]
-
     def order_of(w):
         return (0, 1, 2, 3) if w < 2 else (3, 2, 1, 0)
 
@@ -278,10 +274,33 @@
 
         lax.fori_loop(0, nz - 1, go, 0)
 
+    ld[p] = lg[p]
+    for d in (1, 2, 3):
+        q = (p + d) % 4
+        remote(lg.at[q], ld.at[q], lg_s.at[d - 1], lg_r.at[q], in_plane(d)).wait_recv()
+    whole = ld[0] + ld[1] + ld[2] + ld[3]
+    zl[0] = whole[:, :128]
+    zl[1] = whole[:, 128:]
+
+    relay_wait(len(reaches) - 1)
+
+    decays = [jnp.exp(ld[q]) for q in range(4)]
+
+    def send_decay(k, _):
+        peer = (z + far_first(k, nz)) % nz
+        remote(zl, zd.at[z], zl_s.at[peer], zl_r.at[z], along_z(peer)).start()
+        return 0
+
+    lax.fori_loop(0, nz - 1, send_decay, 0)
+    zd[z] = zl[...]
+
     for w in range(4):
         plane_wait(r1, g1, s1, w)
         combine(w)
         z_send(zs, r2, s2, g2, w)
+
+    feature_copy = remote(features.at[0], features.at[1], f_s.at[0], f_r.at[0], other)
+    feature_copy.start()
 
     scores_t = dot(b_proj, c_proj, 1, 1)
     causal_t = iota((tokens, tokens), 0) <= iota((tokens, tokens), 1)
@@ -378,12 +397,6 @@
     hb[1] = grad_c.astype(BF16)
     for d in (2, 1, 3):
         head_copy(hb, gb, hb_s, hb_r, 1, d).start()
-    gains = []
-    for q in range(4):
-        lanes = slice(256 * q, 256 * q + 256)
-        gains.append(head_sums(dot(c_proj, entering(0, q), 1, 0) * gin[:, lanes].astype(F32)))
-    dr = dr + jnp.concatenate(gains, axis=1)
-
     plane_wait(r5, g5, s5, 2)
     plane_wait(r5, g5, s5, 3)
     for q in range(4):
@@ -391,6 +404,60 @@
     hb[0] = grad_b.astype(BF16)
     for d in (2, 1, 3):
         head_copy(hb, gb, hb_s, hb_r, 0, d).start()
+
+    grad_cs = head_total(hb, gb, hb_s, hb_r, 1).astype(BF16)
+    grad_bs = head_total(hb, gb, hb_s, hb_r, 0).astype(BF16)
+    rounded = jnp.concatenate([grad_bs, grad_cs], axis=1)
+
+    new_row = iota((2 * state, 2 * state), 0)
+    inner = 2 * state // (8 * nz)
+    old_row = (
+        ((new_row // inner) % nz) * (8 * inner)
+        + ((new_row // (inner * nz)) % 2) * (4 * inner)
+        + (new_row // (4 * inner * nz)) * (2 * inner)
+        + ((new_row // (2 * inner * nz)) % 2) * inner
+        + new_row % inner
+    )
+    pick = (iota((2 * state, 2 * state), 1) == old_row).astype(BF16)
+    pt[...] = dot(pick, rounded, 1, 1).astype(BF16)
+    ours = pt[pl.ds(pl.multiple_of(core * state, state), state), :]
+    pair_copy = remote(
+        pt.at[pl.ds(pl.multiple_of((1 - core) * state, state), state)],
+        e1, a1.at[0], b1.at[0], other,
+    )
+    pair_copy.start()
+
+    def y_copy(c, d):
+        return remote(hs.at[c, d - 1], e2.at[c, d - 1], a2.at[c, d - 1], b2.at[c, d - 1], along_y(d))
+
+    feature_copy.wait_recv()
+    pair_copy.wait_recv()
+    both = jnp.concatenate([ours, e1[...]], axis=1)
+    for c in range(CHUNKS):
+        lanes = slice(part * c, part * c + part)
+        fed = jnp.concatenate([features[0, :, lanes], features[1, :, lanes]], axis=0)
+        w1[c] = dot(both, fed, 1, 0)
+        for d in (2, 1, 3):
+            span = pl.ds(pl.multiple_of(((y + d) % 4) * block, block), block)
+            hs[c, d - 1] = w1[c, span, :].astype(BF16)
+            y_copy(c, d).start()
+
+    grad_features[...] = dot(rounded, weight[...], 1, 1).astype(BF16)
+
+    for c in range(CHUNKS):
+        span = pl.ds(pl.multiple_of(y * block, block), block)
+        total = w1[c, span, :]
+        for d in (1, 3, 2):
+            y_copy(c, d).wait_recv()
+            total = total + e2[c, d - 1].astype(F32)
+        for k in range(nz):
+            ws[c, k] = total[2 * k:2 * k + 2].astype(BF16)
+        z_send(ws, e3, a3, b3, c)
+    gains = []
+    for q in range(4):
+        lanes = slice(256 * q, 256 * q + 256)
+        gains.append(head_sums(dot(c_proj, entering(0, q), 1, 0) * gin[:, lanes].astype(F32)))
+    dr = dr + jnp.concatenate(gains, axis=1)
 
     falls, value_dots, kept = [], [], []
     for q in range(4):
@@ -414,53 +481,6 @@
     grads = (jnp.concatenate(value_dots, axis=1) - rate[...] * dlog) * jax.nn.sigmoid(pre)
     grad_dt[...] = jnp.concatenate([grads, jnp.zeros((tokens, 128 - heads), F32)], axis=1).T[:heads]
 
-    grad_cs = head_total(hb, gb, hb_s, hb_r, 1).astype(BF16)
-    grad_bs = head_total(hb, gb, hb_s, hb_r, 0).astype(BF16)
-    rounded = jnp.concatenate([grad_bs, grad_cs], axis=1)
-
-    new_row = iota((2 * state, 2 * state), 0)
-    inner = 2 * state // (8 * nz)
-    old_row = (
-        ((new_row // inner) % nz) * (8 * inner)
-        + ((new_row // (inner * nz)) % 2) * (4 * inner)
-        + (new_row // (4 * inner * nz)) * (2 * inner)
-        + ((new_row // (2 * inner * nz)) % 2) * inner
-        + new_row % inner
-    )
-    pick = (iota((2 * state, 2 * state), 1) == old_row).astype(BF16)
-    pt[...] = dot(pick, rounded, 1, 1).astype(BF16)
-    theirs = pt[pl.ds(pl.multiple_of((1 - core) * state, state), state), :]
-    ours = pt[pl.ds(pl.multiple_of(core * state, state), state), :]
-
-    def pair_copy(c):
-        return remote(w0.at[c], e1.at[c], a1.at[c], b1.at[c], other)
-
-    def y_copy(c, d):
-        return remote(hs.at[c, d - 1], e2.at[c, d - 1], a2.at[c, d - 1], b2.at[c, d - 1], along_y(d))
-
-    for c in range(CHUNKS):
-        w0[c] = dot(theirs, features[:, part * c:part * c + part], 1, 0).astype(BF16)
-        pair_copy(c).start()
-    for c in range(CHUNKS):
-        w1[c] = dot(ours, features[:, part * c:part * c + part], 1, 0)
-    for c in range(CHUNKS):
-        pair_copy(c).wait_recv()
-        for d in (2, 1, 3):
-            span = pl.ds(pl.multiple_of(((y + d) % 4) * block, block), block)
-            hs[c, d - 1] = (w1[c, span, :] + e1[c, span, :].astype(F32)).astype(BF16)
-            y_copy(c, d).start()
-
-    grad_features[...] = dot(rounded, weight[...], 1, 1).astype(BF16)
-
-    for c in range(CHUNKS):
-        span = pl.ds(pl.multiple_of(y * block, block), block)
-        total = w1[c, span, :] + e1[c, span, :].astype(F32)
-        for d in (1, 3, 2):
-            y_copy(c, d).wait_recv()
-            total = total + e2[c, d - 1].astype(F32)
-        for k in range(nz):
-            ws[c, k] = total[2 * k:2 * k + 2].astype(BF16)
-        z_send(ws, e3, a3, b3, c)
     for c in range(CHUNKS):
         z_wait(ws, e3, a3, b3, c)
         total = e3[c, 0].astype(F32)
@@ -479,8 +499,8 @@
             back_copy(w, d).wait_send()
         for c in range(CHUNKS):
             y_copy(c, d).wait_send()
-    for c in range(CHUNKS):
-        pair_copy(c).wait_send()
+    pair_copy.wait_send()
+    feature_copy.wait_send()
 
     def sent(k, _):
         peer = (z + 1 + k) % nz

time: 73.5 us -> 70.9 us (0.965)
  Pallas kernels: 72.7 us -> 70.1 us
    pallas_call x1, Pallas kernels: 71.7 us -> 69.2 us  [per_device(): pl.pallas_call(make_kernel(list(plan)), out_shape=(jax.ShapeDtypeStruct(v...]
where the time goes in v4:
time: 70.9 us; the launch traced here: 70.8 us
  Pallas kernels  70.1 us (99%)
    pallas_call x1, Pallas kernels, per_device(): pl.pallas_call(make_kernel(list(plan)), out_shape=(jax.ShapeDtypeStruct(v...  69.2 us

profile of v4, /device:TPU:1, one launch (start us, length us, event | category | flops | bytes accessed | tf_op | source)
XLA Modules:
  0.0 70.8 jit_solution(8465089595348345559)
XLA Ops:
  0.6 69.2 %layer_backward.1 = (bf16[128,1024]{1,0:T(8,128)(2,1)S(1)}, f32[16,128]{1,0:T(8,128)S(1)}, bf16[128,2048]{1,0:T(8,128)(2,1)S(1)}, f32[2,2048]{1,0:T(2,128)S(1)}) custom-call(bf16[128,1024]{1,0:T(8,128)(2,1)} %bitcast.14, f32[16,128]{1,0:T(8,128)} %bitcast.16, f32[1,16]{1,0:T(1,128)} %bitcast.17, f32[1,16]{1,0:T(1,128)} %bitcast.18, ...), custom_call_target="tpu_custom_call" | custom-call | tf_op jit(solution)/shard_map/layer_backward/pallas_call | solution.py:546
  69.8 0.9 %deliver.1 = (bf16[128,1024]{1,0:T(8,128)(2,1)}, f32[16,128]{1,0:T(8,128)}, bf16[128,2048]{1,0:T(8,128)(2,1)}, f32[2,2048]{1,0:T(2,128)}) custom-call(bf16[128,1024]{1,0:T(8,128)(2,1)S(1)} %get-tuple-element.12.refs_0_, f32[16,128]{1,0:T(8,128)S(1)} %get-tuple-element.13.refs_1_, bf16[128,2048]{1,0:T(8,128)(2,1)S(1)} %get-tuple-element.14.refs_2_, ...), custom_call_target="tpu_custom_call" | custom-call | tf_op jit(solution)/shard_map/deliver/pallas_call | solution.py:529

commit v5 on v4

--- a/solution.py
+++ b/solution.py
@@ -11,7 +11,10 @@
 MESH_ID = pl.DeviceIdType.MESH
 VMEM = pl.BlockSpec(memory_space=pltpu.VMEM)
 HBM = pl.BlockSpec(memory_space=pltpu.HBM)
-CHUNKS = 4
+CHUNKS = 2
+SIDES = 1
+STREAMS = 2 * SIDES
+LANES = 256 // SIDES
 DMA = pltpu.SemaphoreType.DMA
 
 
@@ -62,21 +65,21 @@
         ha_s=DMA((2, 3)), ha_r=DMA((2, 3)), hb_s=DMA((2, 3)), hb_r=DMA((2, 3)),
         lg=pltpu.VMEM((4, 1, 256), F32),
         ld=pltpu.VMEM((4, 1, 256), F32),
-        zl=pltpu.VMEM((2, 1, 128), F32),
-        zd=pltpu.VMEM((nz, 2, 1, 128), F32),
+        zl=pltpu.VMEM((1, 256), F32),
+        zd=pltpu.VMEM((nz, 1, 256), F32),
         lg_s=DMA((3,)), lg_r=DMA((4,)), zl_s=DMA((nz,)), zl_r=DMA((nz,)),
         vin=pltpu.VMEM((tokens, wide), BF16),
         gin=pltpu.VMEM((tokens, wide), BF16),
         sg=pltpu.VMEM((2, 128, wide), BF16),
-        r1=pltpu.VMEM((4, 4, 128, 128), BF16),
-        zs=pltpu.VMEM((4, nz, rows, 128), BF16),
-        r2=pltpu.VMEM((4, nz, rows, 128), BF16),
-        bk=pltpu.VMEM((4, nz, rows, 128), BF16),
-        r4=pltpu.VMEM((4, nz, rows, 128), BF16),
-        p5=pltpu.VMEM((4, 4, 128, 128), BF16),
-        r5=pltpu.VMEM((4, 4, 128, 128), BF16),
-        s1=DMA((4, 3)), g1=DMA((4, 4)), s2=DMA((4, nz)), g2=DMA((4, nz)),
-        s4=DMA((4, nz)), g4=DMA((4, nz)), s5=DMA((4, 3)), g5=DMA((4, 4)),
+        r1=pltpu.VMEM((STREAMS, 4, 128, LANES), BF16),
+        zs=pltpu.VMEM((STREAMS, nz, rows, LANES), BF16),
+        r2=pltpu.VMEM((STREAMS, nz, rows, LANES), BF16),
+        bk=pltpu.VMEM((STREAMS, nz, rows, LANES), BF16),
+        r4=pltpu.VMEM((STREAMS, nz, rows, LANES), BF16),
+        p5=pltpu.VMEM((STREAMS, 4, 128, LANES), BF16),
+        r5=pltpu.VMEM((STREAMS, 4, 128, LANES), BF16),
+        s1=DMA((STREAMS, 3)), g1=DMA((STREAMS, 4)), s2=DMA((STREAMS, nz)), g2=DMA((STREAMS, nz)),
+        s4=DMA((STREAMS, nz)), g4=DMA((STREAMS, nz)), s5=DMA((STREAMS, 3)), g5=DMA((STREAMS, 4)),
         dx=pltpu.VMEM((tokens, wide), F32),
         drow=pltpu.VMEM((tokens, tokens), F32),
         pt=pltpu.VMEM((two_n, tokens), BF16),
@@ -222,8 +225,8 @@
 
     def plane_copy(w, d):
         q = (p + d) % 4
-        lanes = pl.ds(pl.multiple_of(q * 256 + (w % 2) * 128, 128), 128)
-        return remote(sg.at[w // 2, :, lanes], r1.at[w, p], s1.at[w, d - 1], g1.at[w, p], in_plane(d))
+        lanes = pl.ds(pl.multiple_of(q * 256 + (w % SIDES) * LANES, 128), LANES)
+        return remote(sg.at[w // SIDES, :, lanes], r1.at[w, p], s1.at[w, d - 1], g1.at[w, p], in_plane(d))
 
     halves = []
     for i, fed in ((0, vin), (1, gin)):
@@ -231,10 +234,10 @@
         halves.append(total.astype(BF16))
         turned = halves[i].astype(F32).T.astype(BF16)
         sg[i] = dot(turned, fed[...], 1, 0).astype(BF16)
-        for w in (2 * i, 2 * i + 1):
+        for w in range(SIDES * i, SIDES * i + SIDES):
             for d in (2, 3, 1):
                 plane_copy(w, d).start()
-            r1[w, p] = sg[i, :, pl.ds(pl.multiple_of(p * 256 + (w % 2) * 128, 128), 128)]
+            r1[w, p] = sg[i, :, pl.ds(pl.multiple_of(p * 256 + (w % SIDES) * LANES, 128), LANES)]
     b_proj, c_proj = halves
 
     def plane_wait(buf, rs, ss, w):
@@ -242,11 +245,14 @@
             q = (p + d) % 4
             remote(buf.at[w, q], buf.at[w, q], ss.at[w, d - 1], rs.at[w, q], in_plane(d)).wait_recv()
 
+    def lanes_of(w):
+        return slice(LANES * (w % SIDES), LANES * (w % SIDES) + LANES)
+
     def order_of(w):
-        return (0, 1, 2, 3) if w < 2 else (3, 2, 1, 0)
+        return (0, 1, 2, 3) if w < SIDES else (3, 2, 1, 0)
 
     def decay_of(w, q):
-        return decays[q][:, 128 * (w % 2):128 * (w % 2) + 128]
+        return decays[q][:, lanes_of(w)]
 
     def combine(w):
         order = order_of(w)
@@ -278,9 +284,7 @@
     for d in (1, 2, 3):
         q = (p + d) % 4
         remote(lg.at[q], ld.at[q], lg_s.at[d - 1], lg_r.at[q], in_plane(d)).wait_recv()
-    whole = ld[0] + ld[1] + ld[2] + ld[3]
-    zl[0] = whole[:, :128]
-    zl[1] = whole[:, 128:]
+    zl[...] = ld[0] + ld[1] + ld[2] + ld[3]
 
     relay_wait(len(reaches) - 1)
 
@@ -294,7 +298,7 @@
     lax.fori_loop(0, nz - 1, send_decay, 0)
     zd[z] = zl[...]
 
-    for w in range(4):
+    for w in range(STREAMS):
         plane_wait(r1, g1, s1, w)
         combine(w)
         z_send(zs, r2, s2, g2, w)
@@ -337,11 +341,11 @@
     dscore, dcol = local_pairs(0, pairs // 2, dscore, dcol)
 
     def owner_scan(w):
-        carry = jnp.zeros((rows, 128), F32)
+        carry = jnp.zeros((rows, LANES), F32)
         for k in range(nz):
-            m = k if w < 2 else nz - 1 - k
+            m = k if w < SIDES else nz - 1 - k
             bk[w, m] = carry.astype(BF16)
-            carry = carry * jnp.exp(zd[m, w % 2]) + r2[w, m].astype(F32)
+            carry = carry * jnp.exp(zd[m][:, lanes_of(w)]) + r2[w, m].astype(F32)
 
     def decay_wait(k, _):
         peer = (z + 1 + k) % nz
@@ -349,7 +353,7 @@
         return 0
 
     lax.fori_loop(0, nz - 1, decay_wait, 0)
-    for w in range(4):
+    for w in range(STREAMS):
         z_wait(zs, r2, s2, g2, w)
         owner_scan(w)
         z_send(bk, r4, s4, g4, w)
@@ -374,7 +378,7 @@
         q = (p + d) % 4
         return remote(p5.at[w, q], r5.at[w, p], s5.at[w, d - 1], g5.at[w, p], in_plane(d))
 
-    for w in range(4):
+    for w in range(STREAMS):
         z_wait(bk, r4, s4, g4, w)
         expand(w)
         for d in (2, 3, 1):
@@ -388,17 +392,17 @@
         return dot(wide_rows, groups, 1, 0, EXACT)[:, :4]
 
     def entering(i, q):
-        return jnp.concatenate([r5[2 * i, q], r5[2 * i + 1, q]], axis=1)
-
-    plane_wait(r5, g5, s5, 0)
-    plane_wait(r5, g5, s5, 1)
+        return jnp.concatenate([r5[SIDES * i + n, q] for n in range(SIDES)], axis=1)
+
+    for w in range(SIDES):
+        plane_wait(r5, g5, s5, w)
     for q in range(4):
         grad_c = grad_c + dot(gin[:, 256 * q:256 * q + 256], entering(0, q), 1, 1)
     hb[1] = grad_c.astype(BF16)
     for d in (2, 1, 3):
         head_copy(hb, gb, hb_s, hb_r, 1, d).start()
-    plane_wait(r5, g5, s5, 2)
-    plane_wait(r5, g5, s5, 3)
+    for w in range(SIDES, STREAMS):
+        plane_wait(r5, g5, s5, w)
     for q in range(4):
         grad_b = grad_b + dot(vin[:, 256 * q:256 * q + 256], entering(1, q), 1, 1)
     hb[0] = grad_b.astype(BF16)
@@ -494,7 +498,7 @@
             head_copy(ha, ga, ha_s, ha_r, i, d).wait_send()
             head_copy(hb, gb, hb_s, hb_r, i, d).wait_send()
         remote(lg.at[q], ld.at[p], lg_s.at[d - 1], lg_r.at[p], in_plane(d)).wait_send()
-        for w in range(4):
+        for w in range(STREAMS):
             plane_copy(w, d).wait_send()
             back_copy(w, d).wait_send()
         for c in range(CHUNKS):
@@ -506,7 +510,7 @@
         peer = (z + 1 + k) % nz
         where = along_z(peer)
         remote(zl, zd.at[z], zl_s.at[peer], zl_r.at[z], where).wait_send()
-        for w in range(4):
+        for w in range(STREAMS):
             remote(zs.at[w, peer], r2.at[w, z], s2.at[w, peer], g2.at[w, z], where).wait_send()
             remote(bk.at[w, peer], r4.at[w, z], s4.at[w, peer], g4.at[w, z], where).wait_send()
         for c in range(CHUNKS):

time: 70.9 us -> 69.7 us (0.983)
  Pallas kernels: 70.1 us -> 68.9 us
    pallas_call x1, Pallas kernels: 69.2 us -> 67.9 us  [per_device(): pl.pallas_call(make_kernel(list(plan)), out_shape=(jax.ShapeDtypeStruct(v...]
where the time goes in v5:
time: 69.7 us; the launch traced here: 69.5 us
  Pallas kernels  68.9 us (99%)
    pallas_call x1, Pallas kernels, per_device(): pl.pallas_call(make_kernel(list(plan)), out_shape=(jax.ShapeDtypeStruct(v...  67.9 us

profile of v5, /device:TPU:1, one launch (start us, length us, event | category | flops | bytes accessed | tf_op | source)
XLA Modules:
  0.0 69.5 jit_solution(10559071366804829398)
XLA Ops:
  0.6 67.9 %layer_backward.1 = (bf16[128,1024]{1,0:T(8,128)(2,1)S(1)}, f32[16,128]{1,0:T(8,128)S(1)}, bf16[128,2048]{1,0:T(8,128)(2,1)S(1)}, f32[2,2048]{1,0:T(2,128)S(1)}) custom-call(bf16[128,1024]{1,0:T(8,128)(2,1)} %bitcast.14, f32[16,128]{1,0:T(8,128)} %bitcast.16, f32[1,16]{1,0:T(1,128)} %bitcast.17, f32[1,16]{1,0:T(1,128)} %bitcast.18, ...), custom_call_target="tpu_custom_call" | custom-call | tf_op jit(solution)/shard_map/layer_backward/pallas_call | solution.py:550
  68.6 0.9 %deliver.1 = (bf16[128,1024]{1,0:T(8,128)(2,1)}, f32[16,128]{1,0:T(8,128)}, bf16[128,2048]{1,0:T(8,128)(2,1)}, f32[2,2048]{1,0:T(2,128)}) custom-call(bf16[128,1024]{1,0:T(8,128)(2,1)S(1)} %get-tuple-element.12.refs_0_, f32[16,128]{1,0:T(8,128)S(1)} %get-tuple-element.13.refs_1_, bf16[128,2048]{1,0:T(8,128)(2,1)S(1)} %get-tuple-element.14.refs_2_, ...), custom_call_target="tpu_custom_call" | custom-call | tf_op jit(solution)/shard_map/deliver/pallas_call | solution.py:533

commit v6 on v5

--- a/solution.py
+++ b/solution.py
@@ -56,7 +56,7 @@
         features=pltpu.VMEM((2, tokens, feats), BF16),
         weight=pltpu.VMEM((feats, two_n), BF16),
         out_grad=pltpu.VMEM((tokens, wide), BF16),
-        fetched=DMA((7,)),
+        fetched=DMA((9,)),
         relay=pltpu.SemaphoreType.REGULAR((max(nz.bit_length() - 2, 1),)),
         ha=pltpu.VMEM((2, tokens, two_n // 2), BF16),
         hb=pltpu.VMEM((2, tokens, two_n // 2), BF16),
@@ -82,6 +82,7 @@
         s4=DMA((STREAMS, nz)), g4=DMA((STREAMS, nz)), s5=DMA((STREAMS, 3)), g5=DMA((STREAMS, 4)),
         dx=pltpu.VMEM((tokens, wide), F32),
         drow=pltpu.VMEM((tokens, tokens), F32),
+        pick=pltpu.VMEM((two_n, two_n), BF16),
         pt=pltpu.VMEM((two_n, tokens), BF16),
         w1=pltpu.VMEM((CHUNKS, two_n // 2, part), F32),
         e1=pltpu.VMEM((two_n // 2, tokens), BF16),
@@ -105,13 +106,22 @@
          ha, hb, ga, gb, ha_s, ha_r, hb_s, hb_r,
          lg, ld, zl, zd, lg_s, lg_r, zl_s, zl_r,
          vin, gin, sg, r1, zs, r2, bk, r4, p5, r5, s1, g1, s2, g2, s4, g4, s5, g5,
-         dx, drow, pt, w1, e1, hs, e2, ws, e3, f_s, f_r, a1, b1, a2, b2, a3, b3):
+         dx, drow, pick, pt, w1, e1, hs, e2, ws, e3, f_s, f_r, a1, b1, a2, b2, a3, b3):
     grad_values, grad_dt, grad_features, grad_weight = results
     here = (values, raw_t, bias, rate, features.at[0], weight, out_grad)
-    fetches = [
-        pltpu.make_async_copy(held[i], here[i], fetched.at[i]) for i in range(7)
-    ]
-    for i in (5, 4, 1, 2, 3, 0, 6):
+    fetches = {
+        i: pltpu.make_async_copy(held[i], here[i], fetched.at[i]) for i in (0, 1, 2, 3, 6)
+    }
+    deep = weight.shape[0] // 2
+    for n in range(2):
+        down, across = pl.ds(deep * n, deep), pl.ds(deep * n, deep)
+        fetches[4, n] = pltpu.make_async_copy(
+            held[4].at[:, across], here[4].at[:, across], fetched.at[4 + 3 * n]
+        )
+        fetches[5, n] = pltpu.make_async_copy(
+            held[5].at[down], here[5].at[down], fetched.at[5 + 3 * n]
+        )
+    for i in ((4, 0), (5, 0), (4, 1), (5, 1), 1, 2, 3, 0, 6):
         fetches[i].start()
     ctx, head, dp = lax.axis_index("ctx"), lax.axis_index("head"), lax.axis_index("dp")
     nz = zd.shape[0]
@@ -149,9 +159,13 @@
         greet(barrier, along_y(d))
         greet(barrier, in_plane(d))
 
-    fetches[5].wait()
-    fetches[4].wait()
-    partial = dot(features[0], weight[...], 1, 0).astype(BF16)
+    sums = 0.0
+    for n in range(2):
+        fetches[4, n].wait()
+        fetches[5, n].wait()
+        span = slice(deep * n, deep * n + deep)
+        sums = sums + dot(features[0, :, span], weight[span, :], 1, 0)
+    partial = sums.astype(BF16)
     ha[0] = partial[:, :state]
     ha[1] = partial[:, state:]
 
@@ -365,6 +379,17 @@
     grad_c = dot(dscore_n, b_proj, 1, 0)
     dr = drow[...].T[:, :heads] - dcol
 
+    new_row = iota((2 * state, 2 * state), 0)
+    inner = 2 * state // (8 * nz)
+    old_row = (
+        ((new_row // inner) % nz) * (8 * inner)
+        + ((new_row // (inner * nz)) % 2) * (4 * inner)
+        + (new_row // (4 * inner * nz)) * (2 * inner)
+        + ((new_row // (2 * inner * nz)) % 2) * inner
+        + new_row % inner
+    )
+    pick[...] = (iota((2 * state, 2 * state), 1) == old_row).astype(BF16)
+
     def expand(w):
         for j in range(nz):
             span = slice(j * rows, j * rows + rows)
@@ -410,20 +435,11 @@
         head_copy(hb, gb, hb_s, hb_r, 0, d).start()
 
     grad_cs = head_total(hb, gb, hb_s, hb_r, 1).astype(BF16)
+    picked = dot(pick[:, state:], grad_cs, 1, 1)
     grad_bs = head_total(hb, gb, hb_s, hb_r, 0).astype(BF16)
     rounded = jnp.concatenate([grad_bs, grad_cs], axis=1)
 
-    new_row = iota((2 * state, 2 * state), 0)
-    inner = 2 * state // (8 * nz)
-    old_row = (
-        ((new_row // inner) % nz) * (8 * inner)
-        + ((new_row // (inner * nz)) % 2) * (4 * inner)
-        + (new_row // (4 * inner * nz)) * (2 * inner)
-        + ((new_row // (2 * inner * nz)) % 2) * inner
-        + new_row % inner
-    )
-    pick = (iota((2 * state, 2 * state), 1) == old_row).astype(BF16)
-    pt[...] = dot(pick, rounded, 1, 1).astype(BF16)
+    pt[...] = (picked + dot(pick[:, :state], grad_bs, 1, 1)).astype(BF16)
     ours = pt[pl.ds(pl.multiple_of(core * state, state), state), :]
     pair_copy = remote(
         pt.at[pl.ds(pl.multiple_of((1 - core) * state, state), state)],

time: 69.7 us -> 69.9 us (level); the launches traced: 69.5 us -> 69 us
  no operation moved by 1% of the time
where the time goes in v6:
time: 69.9 us; the launch traced here: 69 us
  Pallas kernels  68.3 us (98%)
    pallas_call x1, Pallas kernels, per_device(): pl.pallas_call(make_kernel(list(plan)), out_shape=(jax.ShapeDtypeStruct(v...  67.4 us

profile of v6, /device:TPU:1, one launch (start us, length us, event | category | flops | bytes accessed | tf_op | source)
XLA Modules:
  0.0 69.0 jit_solution(3348013101655096548)
XLA Ops:
  0.6 67.4 %layer_backward.1 = (bf16[128,1024]{1,0:T(8,128)(2,1)S(1)}, f32[16,128]{1,0:T(8,128)S(1)}, bf16[128,2048]{1,0:T(8,128)(2,1)S(1)}, f32[2,2048]{1,0:T(2,128)S(1)}) custom-call(bf16[128,1024]{1,0:T(8,128)(2,1)} %bitcast.14, f32[16,128]{1,0:T(8,128)} %bitcast.16, f32[1,16]{1,0:T(1,128)} %bitcast.17, f32[1,16]{1,0:T(1,128)} %bitcast.18, ...), custom_call_target="tpu_custom_call" | custom-call | tf_op jit(solution)/shard_map/layer_backward/pallas_call | solution.py:566
  68.1 0.9 %deliver.1 = (bf16[128,1024]{1,0:T(8,128)(2,1)}, f32[16,128]{1,0:T(8,128)}, bf16[128,2048]{1,0:T(8,128)(2,1)}, f32[2,2048]{1,0:T(2,128)}) custom-call(bf16[128,1024]{1,0:T(8,128)(2,1)S(1)} %get-tuple-element.12.refs_0_, f32[16,128]{1,0:T(8,128)S(1)} %get-tuple-element.13.refs_1_, bf16[128,2048]{1,0:T(8,128)(2,1)S(1)} %get-tuple-element.14.refs_2_, ...), custom_call_target="tpu_custom_call" | custom-call | tf_op jit(solution)/shard_map/deliver/pallas_call | solution.py:549
